TPU v7x, 256 devices: a whole 4x4x8 slice. The times are simulated.
256 devices in a mesh: seq: 16 (over x_hi, y, core), tp: 16 (over z, x_lo).
Axes of the slice: x: 4 (x_hi: 2, x_lo: 2; x = x_hi * 2 + x_lo), y: 4, z: 8, core: 2. Of those that a mesh axis runs over, the one named last changes fastest.
Arguments:
- hidden: bfloat16 [12288, 8192], P('seq', 'tp'), may hold values from -6 to 6
- cotangent: bfloat16 [12288, 8192], P('seq', 'tp'), may hold values from -0.59765625 to 0.59765625
- router_gate: bfloat16 [12288], P('seq'), may hold values from 0.25 to 1
- recursion_depth: int32 [12288], P('seq'), may hold values from 1 to 4
- live_counts: int32 [16], replicated, may hold values from 0 to 768, as said below
- out_weight: bfloat16 [8192, 8192], P(None, 'tp'), may hold values from -0.0625 to 0.0625
- adapter_down: bfloat16 [8192, 1024], P('tp', 'seq'), may hold values from -0.0625 to 0.0625
- adapter_up: bfloat16 [1024, 8192], P('seq', 'tp'), may hold values from -0.375 to 0.375
Outputs:
- hidden_grad: float32 [12288, 8192], P('seq', 'tp')
- gate_grad: float32 [12288], P('seq')
- weight_grad: float32 [8192, 8192], P('seq', 'tp')
- down_grad: float32 [1024, 8192], P('seq', 'tp')
- up_grad: float32 [1024, 8192], P('seq', 'tp')
Inputs may be any that keep to these rules, and one draw needn't show every extreme that they name: `live_counts`: each entry is a multiple of 128; the entries sum to 6144; the largest entry equals 768. Rows at or past an index's count are not live.
All inputs are finite; a program needn't handle non-finite values.
Results may differ from a plain program's by a relative error of at most 0.0055.
Values may be sent and summed in bfloat16 or wider, within the bound.
A program may use at most 192 MiB of HBM per device.

v0:
```python
import jax
import jax.numpy as jnp
from jax import lax
from jax.sharding import PartitionSpec as P

NREC = 4
BAL = 384


adapter_scale = 0.5
contract_rows = (((0,), (0,)), ((), ()))
contract_last = (((1,), (1,)), ((), ()))


def select_block(wide_values, selector):
    row_total = wide_values.shape[0]
    return jnp.sum(
        wide_values.reshape(row_total, selector.shape[1], -1) * selector[:, :, None], axis=1
    )


def spread_block(values, selector):
    return (selector[:, :, None] * values[:, None, :]).reshape(values.shape[0], -1)


def local(
    hidden,
    cotangent,
    router_gate,
    recursion_depth,
    live_counts,
    out_weight,
    adapter_down,
    adapter_up,
):
    shards = lax.axis_size("seq")
    slot_count = hidden.shape[0]
    width_local = hidden.shape[1]
    per_pair = slot_count // shards
    shares = live_counts // shards
    finish = jnp.cumsum(shares)
    starts_at = finish - shares
    shard_ids = jnp.arange(shards, dtype=jnp.int32)
    adapters_down, adapters_up = (
        lax.all_gather(adapter_down, "seq", axis=1, tiled=True),
        lax.all_gather(adapter_up, "seq", axis=0, tiled=True),
    )
    rank_slots = jnp.arange(BAL, dtype=jnp.int32)
    source = jnp.sum((finish[None, :] <= rank_slots[:, None]).astype(jnp.int32), axis=1)
    begin_at = jnp.sum(
        jnp.where(source[:, None] == shard_ids[None, :], starts_at[None, :], 0), axis=1
    )
    pick_rows = (rank_slots - begin_at) * shards + source
    arrived = (
        lax.all_to_all(
            hidden.reshape(per_pair, shards, width_local),
            "seq",
            split_axis=1,
            concat_axis=1,
            tiled=True,
        ),
        lax.all_to_all(
            cotangent.reshape(per_pair, shards, width_local),
            "seq",
            split_axis=1,
            concat_axis=1,
            tiled=True,
        ),
        lax.all_to_all(
            router_gate.reshape(per_pair, shards), "seq", split_axis=1, concat_axis=1, tiled=True
        ),
        lax.all_to_all(
            recursion_depth.astype(jnp.bfloat16).reshape(per_pair, shards),
            "seq",
            split_axis=1,
            concat_axis=1,
            tiled=True,
        ),
    )
    rows_h = jnp.take(arrived[0].reshape(slot_count, width_local), pick_rows, axis=0)
    rows_dy = jnp.take(arrived[1].reshape(slot_count, width_local), pick_rows, axis=0)
    gate_rows = jnp.take(arrived[2].reshape(slot_count), pick_rows).astype(jnp.float32)
    depths = jnp.take(arrived[3].reshape(slot_count), pick_rows).astype(jnp.float32)
    live_mask = jnp.ones((BAL,), dtype=bool)
    levels = jnp.arange(1, NREC + 1, dtype=jnp.float32)
    selector = (depths[:, None] == levels[None, :]).astype(jnp.float32)
    full_dy = lax.all_gather(rows_dy, "tp", axis=1, tiled=True)
    gated_dy = (gate_rows[:, None] * full_dy).astype(jnp.bfloat16)
    down_part = jnp.dot(rows_h, adapters_down, preferred_element_type=jnp.float32)
    up_part = lax.dot_general(
        rows_dy, adapters_up, contract_last, preferred_element_type=jnp.float32
    )
    down_proj, up_summed = lax.psum(
        (select_block(down_part, selector), select_block(up_part, selector)), "tp"
    )
    up_back = adapter_scale * up_summed
    wide_back = spread_block(up_back, selector)
    wide_down = spread_block(down_proj, selector)
    pre_grad = jnp.dot(full_dy, out_weight, preferred_element_type=jnp.float32)
    pre_grad = pre_grad + lax.dot_general(
        wide_back.astype(jnp.bfloat16),
        adapters_down,
        contract_last,
        preferred_element_type=jnp.float32,
    )
    row_grad = gate_rows[:, None] * pre_grad
    gate_part = jnp.sum(rows_h.astype(jnp.float32) * pre_grad, axis=1)
    gate_total = lax.psum(gate_part, "tp")
    gate_row = jnp.where(live_mask, gate_total, 0.0)
    back_gated = (gate_rows[:, None] * wide_back).astype(jnp.bfloat16)
    down_gated = (gate_rows[:, None] * adapter_scale * wide_down).astype(jnp.bfloat16)
    down_local = lax.dot_general(
        back_gated, rows_h, contract_rows, preferred_element_type=jnp.float32
    )
    up_local = lax.dot_general(
        down_gated, rows_dy, contract_rows, preferred_element_type=jnp.float32
    )
    down_grad, up_grad = (
        lax.psum_scatter(down_local, "seq", scatter_dimension=0, tiled=True),
        lax.psum_scatter(up_local, "seq", scatter_dimension=0, tiled=True),
    )
    weight_grad = lax.psum_scatter(
        lax.dot_general(gated_dy, rows_h, contract_rows, preferred_element_type=jnp.float32),
        "seq",
        scatter_dimension=0,
        tiled=True,
    )
    position = jnp.arange(slot_count, dtype=jnp.int32)
    within = position // shards
    owner_shard = position % shards
    owner_pick = owner_shard[:, None] == shard_ids[None, :]
    alive_mask = within < jnp.sum(jnp.where(owner_pick, shares[None, :], 0), axis=1)
    back_rows = jnp.where(
        alive_mask, jnp.sum(jnp.where(owner_pick, starts_at[None, :], 0), axis=1) + within, 0
    )
    grad_slots = jnp.where(alive_mask[:, None], jnp.take(row_grad, back_rows, axis=0), 0.0)
    gate_slots = jnp.where(alive_mask, jnp.take(gate_row, back_rows), 0.0)
    returned = (
        lax.all_to_all(
            grad_slots.reshape(per_pair, shards, width_local),
            "seq",
            split_axis=1,
            concat_axis=1,
            tiled=True,
        ),
        lax.all_to_all(
            gate_slots.reshape(per_pair, shards), "seq", split_axis=1, concat_axis=1, tiled=True
        ),
    )
    hidden_grad = returned[0].reshape(slot_count, width_local)
    gate_grad = returned[1].reshape(slot_count)
    return (hidden_grad, gate_grad, weight_grad, down_grad, up_grad)


def solution(mesh):
    in_specs = (
        P("seq", "tp"),
        P("seq", "tp"),
        P("seq"),
        P("seq"),
        P(),
        P(None, "tp"),
        P("tp", "seq"),
        P("seq", "tp"),
    )
    out_specs = (P("seq", "tp"), P("seq"), P("seq", "tp"), P("seq", "tp"), P("seq", "tp"))
    return jax.shard_map(local, mesh=mesh, in_specs=in_specs, out_specs=out_specs, check_vma=False)
```

profile of v0, /device:TPU:4, one launch (start us, length us, event | category | flops | bytes accessed | tf_op | source)
XLA Modules:
  0.0 740.8 jit_solution(5156661146173279528)
XLA Ops:
  7.2 0.7 all-gather.6.cloned.1.call-update
  7.9 0.7 convert_element_type.39
  8.7 0.7 copy.64
  9.4 7.5 %all-to-all-start.2 = ((bf16[48,16,1]{0,2,1:T(2,128)(2,1)}), bf16[48,16,1]{0,2,1:T(2,128)(2,1)S(1)}, u32[]{:S(2)}, u32[]{:S(2)}) async-start(bf16[48,16,1]{0,2,1:T(2,128)(2,1)} %copy.64), calls=%async_computation.2 | async-start | bytes 16384 | tf_op jit(solution)/shard_map/all_to_all | solution.py:72
  16.9 0.7 all-gather.8.cloned.1.call-update
  17.6 0.8 all_to_all.25
  18.4 0.7 copy.60
  19.0 2.4 all-to-all-done.2
  21.5 6.3 all-to-all-start
  27.7 0.7 fusion.29
  28.7 2.4 copy.69
  31.1 1.3 copy.62
  32.4 7.3 all-to-all-start.4
  39.9 12.4 %all-to-all-done.4 = bf16[48,16,512]{2,0,1:T(8,128)(2,1)S(1)} async-done(((bf16[48,16,512]{2,0,1:T(8,128)(2,1)}), bf16[48,16,512]{2,0,1:T(8,128)(2,1)S(1)}, u32[]{:S(2)}, u32[]{:S(2)}) %all-to-all-start.4) | async-done | bytes 786464 | tf_op jit(solution)/shard_map/all_to_all | solution.py:55
  52.3 6.4 all-to-all-start.1
  59.1 2.8 gather_fusion.4
  61.9 2.8 gather_fusion.2
  64.9 0.8 copy.66
  66.1 2.1 gather_fusion.5
  68.2 2.8 all-to-all-done.1
  71.4 2.1 gather_fusion.3
  73.7 0.7 copy-done
  74.4 1.8 fusion.20
  76.2 0.7 reshape.383
  77.0 36.6 %all-gather.8.cloned.1.call-done = bf16[512,1024]{0,1:T(8,128)(2,1)} async-done(((bf16[512,64]{0,1:T(8,128)(2,1)}), bf16[512,1024]{0,1:T(8,128)(2,1)}) %all-gather.8.cloned.1.call-update) | async-done | bytes 1048592 | tf_op jit(solution)/shard_map/all_gather | solution.py:45
  113.5 1.8 fusion.17
  115.4 1.9 reshape.388
  117.2 4.3 multiply_reduce_fusion
  122.1 139.8 %all-reduce.3.cloned.1.call-done = (f32[384,256]{1,0:T(8,128)}, f32[384,256]{1,0:T(8,128)}) async-done(((f32[384,256]{1,0:T(8,128)}, f32[384,256]{1,0:T(8,128)}), (f32[384,256]{1,0:T(8,128)}, f32[384,256]{1,0:T(8,128)})) %all-reduce.3.cloned.1.call-update) | async-done | bytes 786448 | tf_op jit(solution)/shard_map/psum | solution.py:93
  262.0 1.0 broadcast_multiply_fusion.3
  263.0 1.7 broadcast_multiply_fusion
  265.7 2.2 fusion.4
  268.5 2.2 fusion.3
  270.7 134.1 %all-gather.4.cloned.1.call-done = bf16[384,8192]{1,0:T(8,128)(2,1)} async-done(((bf16[384,512]{1,0:T(8,128)(2,1)}), bf16[384,8192]{1,0:T(8,128)(2,1)}) %all-gather.4.cloned.1.call-update) | async-done | bytes 6291472 | tf_op jit(solution)/shard_map/all_gather | solution.py:87
  404.8 11.3 %fusion = f32[8192,512]{1,0:T(8,128)} fusion(bf16[384,8192]{1,0:T(8,128)(2,1)} %all-gather.4.cloned.1.call-done, f32[384]{0:T(512)S(1)} %get-tuple-element.21, bf16[384,512]{1,0:T(8,128)(2,1)S(1)} %gather_fusion.5, pred[384]{0:T(512)(128)(4,1)S(1)} %get-tuple-element.14), kind=kOutput, calls=%fused_computation.7 | convolution fusion | flops 3230859264 | bytes 23463808 | tf_op jit(solution)/shard_map/dot_general | solution.py:123
  417.4 7.9 %fusion.19 = f32[384,512]{1,0:T(8,128)S(1)} fusion(bf16[384,8192]{1,0:T(8,128)(2,1)} %all-gather.4.cloned.1.call-done, bf16[8192,512]{1,0:T(8,128)(2,1)} %param.17), kind=kOutput, calls=%fused_computation.80 | convolution fusion | flops 3221225472 | bytes 15466496 | tf_op jit(solution)/shard_map/dot_general | solution.py:99
  425.3 0.7 multiply_reduce_fusion.2
  426.0 33.1 %psum.22 = f32[384]{0:T(512)S(1)} all-reduce(f32[384]{0:T(512)S(1)} %get-tuple-element.17), channel_id=1, replica_groups=mesh['seq'=16,'tp'=16] {'tp'}, use_global_device_ids=true, to_apply=%region_8.11 | all-reduce | flops 384 | bytes 3072 | tf_op jit(solution)/shard_map/psum | solution.py:108
  459.1 5.0 gather_fusion.1
  464.9 7.3 all-to-all-start.5
  472.2 2.2 gather_fusion
  474.3 2.2 fusion.2
  476.9 6.9 all-to-all-start.3
  483.9 0.7 reshape.387
  484.6 20.1 %all-to-all-done.3 = f32[48,16,512]{2,0,1:T(8,128)S(1)} async-done(((f32[48,16,512]{2,0,1:T(8,128)}), f32[48,16,512]{2,0,1:T(8,128)S(1)}, u32[]{:S(2)}, u32[]{:S(2)}) %all-to-all-start.3) | async-done | bytes 1572896 | tf_op jit(solution)/shard_map/all_to_all | solution.py:139
  504.6 2.1 copy.68
  506.7 69.5 %reduce-scatter.6.cloned.1.call-done = f32[64,512]{1,0:T(8,128)} async-done(((f32[1024,512]{1,0:T(8,128)}), f32[64,512]{1,0:T(8,128)}) %reduce-scatter.6.cloned.1.call-update) | async-done | bytes 131088 | tf_op jit(solution)/shard_map/reduce_scatter | solution.py:119
  576.2 157.8 %reduce-scatter.4.cloned.1.call-done = f32[512,512]{1,0:T(8,128)} async-done(((f32[8192,512]{1,0:T(8,128)}), f32[512,512]{1,0:T(8,128)}) %reduce-scatter.4.cloned.1.call-update) | async-done | bytes 1048592 | tf_op jit(solution)/shard_map/reduce_scatter | solution.py:122
  (67 shorter events, 6.8 us)
Async XLA Ops:
  7.2 23.9 %copy-start.4 = (bf16[768,512]{1,0:T(8,128)(2,1)S(1)}, bf16[768,512]{1,0:T(8,128)(2,1)}, u32[]{:S(2)}) copy-start(bf16[768,512]{1,0:T(8,128)(2,1)} %param.13) | copy-start | bytes 2359300
  7.2 66.5 %all-gather.6.cloned.1.call-start = ((), (), s32[]{:S(2)}) async-start(), calls=%async_computation.10 | async-start | bytes 1114112 | tf_op jit(solution)/shard_map/all_gather | solution.py:46
  9.4 12.1 %all-to-all-start.2 = ((bf16[48,16,1]{0,2,1:T(2,128)(2,1)}), bf16[48,16,1]{0,2,1:T(2,128)(2,1)S(1)}, u32[]{:S(2)}, u32[]{:S(2)}) async-start(bf16[48,16,1]{0,2,1:T(2,128)(2,1)} %copy.64), calls=%async_computation.2 | async-start | bytes 16384 | tf_op jit(solution)/shard_map/all_to_all | solution.py:72
  16.8 96.7 %all-gather.8.cloned.1.call-start = ((), (), s32[]{:S(2)}) async-start(), calls=%async_computation.11 | async-start | bytes 1114112 | tf_op jit(solution)/shard_map/all_gather | solution.py:45
  21.5 10.9 %all-to-all-start = ((bf16[48,16,1]{0,2,1:T(2,128)(2,1)}), bf16[48,16,1]{0,2,1:T(2,128)(2,1)S(1)}, u32[]{:S(2)}, u32[]{:S(2)}) async-start(bf16[48,16,1]{0,2,1:T(2,128)(2,1)} %copy.60), calls=%async_computation | async-start | bytes 16384 | tf_op jit(solution)/shard_map/all_to_all | solution.py:69
  31.1 8.7 %copy-start.5 = (s32[16]{0:T(128)S(1)}, s32[16]{0:T(128)}, u32[]{:S(2)}) copy-start(s32[16]{0:T(128)} %param.16) | copy-start | bytes 196
  32.4 19.9 %all-to-all-start.4 = ((bf16[48,16,512]{2,0,1:T(8,128)(2,1)}), bf16[48,16,512]{2,0,1:T(8,128)(2,1)S(1)}, u32[]{:S(2)}, u32[]{:S(2)}) async-start(bf16[48,16,512]{2,0,1:T(8,128)(2,1)} %copy.69), calls=%async_computation.4 | async-start | bytes 1572864 | tf_op jit(solution)/shard_map/all_to_all | solution.py:55
  52.3 18.7 %all-to-all-start.1 = ((bf16[48,16,512]{2,0,1:T(8,128)(2,1)}), bf16[48,16,512]{2,0,1:T(8,128)(2,1)S(1)}, u32[]{:S(2)}, u32[]{:S(2)}) async-start(bf16[48,16,512]{2,0,1:T(8,128)(2,1)} %copy.62), calls=%async_computation.1 | async-start | bytes 1572864 | tf_op jit(solution)/shard_map/all_to_all | solution.py:62
  58.7 203.3 %all-reduce.3.cloned.1.call-start = ((), (), s32[]{:S(2)}) async-start(), calls=%async_computation.15 | async-start | bytes 1572864 | tf_op jit(solution)/shard_map/psum | solution.py:93
  73.6 0.7 copy-start
  121.5 141.5 %copy-start.3 = (f32[384,4]{1,0:T(8,128)S(1)}, f32[384,4]{1,0:T(8,128)}, u32[]{:S(2)}) copy-start(f32[384,4]{1,0:T(8,128)} %copy.66) | copy-start | bytes 18436
  121.5 283.3 %all-gather.4.cloned.1.call-start = ((), (), s32[]{:S(2)}) async-start(), calls=%async_computation.9 | async-start | bytes 6684672 | tf_op jit(solution)/shard_map/all_gather | solution.py:87
  122.1 384.6 %reduce-scatter.8.cloned.1.call-start = ((), (), s32[]{:S(2)}) async-start(), calls=%async_computation.14 | async-start | bytes 2228224 | tf_op jit(solution)/shard_map/reduce_scatter | solution.py:120
  264.7 1.0 copy-start.1
  267.9 308.3 %reduce-scatter.6.cloned.1.call-start = ((), (), s32[]{:S(2)}) async-start(), calls=%async_computation.13 | async-start | bytes 2228224 | tf_op jit(solution)/shard_map/reduce_scatter | solution.py:119
  270.7 463.2 %reduce-scatter.4.cloned.1.call-start = ((), (), s32[]{:S(2)}) async-start(), calls=%async_computation.12 | async-start | bytes 17825792 | tf_op jit(solution)/shard_map/reduce_scatter | solution.py:122
  416.1 0.7 copy-start.6
  417.4 7.9 %copy-start.2 = (bf16[512,1024]{0,1:T(8,128)(2,1)S(1)}, bf16[512,1024]{0,1:T(8,128)(2,1)}, u32[]{:S(2)}) copy-start(bf16[512,1024]{0,1:T(8,128)(2,1)} %all-gather.8.cloned.1.call-done) | copy-start | bytes 3145732
  464.9 12.0 %all-to-all-start.5 = ((f32[48,16,1]{0,2,1:T(1,128)}), f32[48,16,1]{0,2,1:T(1,128)S(1)}, u32[]{:S(2)}, u32[]{:S(2)}) async-start(f32[48,16,1]{0,2,1:T(1,128)} %copy.71), calls=%async_computation.5 | async-start | bytes 16384 | tf_op jit(solution)/shard_map/all_to_all | solution.py:146
  476.9 27.7 %all-to-all-start.3 = ((f32[48,16,512]{2,0,1:T(8,128)}), f32[48,16,512]{2,0,1:T(8,128)S(1)}, u32[]{:S(2)}, u32[]{:S(2)}) async-start(f32[48,16,512]{2,0,1:T(8,128)} %fusion.2), calls=%async_computation.3 | async-start | bytes 3145728 | tf_op jit(solution)/shard_map/all_to_all | solution.py:139
Sparse Core Ops, SparseCore 0:
  10.7 50.5 all-gather.5
  64.1 49.3 all-gather.7
  121.6 140.2 all-reduce.2
  264.2 140.6 all-gather.3
  409.4 78.6 reduce-scatter.7
  492.8 83.3 reduce-scatter.5
  581.3 152.5 reduce-scatter.3
where the time goes:
time: 744 us; the launch traced here: 741 us
  waiting for transfers between devices  578 us (78%)
  starting transfers between devices  42 us (6%)
  local copies, waits for them, and re-layouts  34.3 us (5%)
  blocking collectives  33.1 us (4%)
  matrix products  27.9 us (4%)
  between operations  14.4 us (2%)
  other arithmetic  11.4 us (2%)
    reduce_scatter x1, waiting for transfers between devices, local(): lax.psum_scatter(lax.dot_general(gated_dy, rows_h, contract_rows, preferr...  158 us
    psum x1, waiting for transfers between devices, local(): lax.psum((select_block(down_part, selector), select_block(up_part, select...  140 us
    all_gather x1, waiting for transfers between devices, local(): full_dy = lax.all_gather(rows_dy, 'tp', axis=1, tiled=True)  134 us
    reduce_scatter x1, waiting for transfers between devices, local(): lax.psum_scatter(down_local, 'seq', scatter_dimension=0, tiled=True)  69.5 us
    all_gather x1, waiting for transfers between devices, local(): lax.all_gather(adapter_down, 'seq', axis=1, tiled=True)  36.6 us
    psum x1, blocking collectives, local(): gate_total = lax.psum(gate_part, 'tp')  33.1 us
    all_to_all x1, waiting for transfers between devices, local(): lax.all_to_all(grad_slots.reshape(per_pair, shards, width_local), 'seq',...  20.1 us
  transfers between devices with their start and end apart: 13, of which 10 were waited for; matrix products, arithmetic and copies ran while one was open for 8% of the time, Pallas kernels for 0%

commit v1 on v0

v1 whole, which is shorter than its diff:
```python
import jax
import jax.numpy as jnp
from jax import lax
from jax.experimental import pallas as pl
from jax.experimental.pallas import tpu as pltpu
from jax.sharding import PartitionSpec as P

NREC = 4
BLOCK = 128
GROUP = 16
CHIPS = 8
LEVELS = 6
GROUPS = 48
ROWS = GROUPS * GROUP
RING = 8
HALF = GROUPS // 2
WIDTH = 512
RANK = 256
PART = 48
PEERS = 16
VMEM_LIMIT = 60 * 1024 * 1024

contract_rows = (((0,), (0,)), ((), ()))
contract_last = (((1,), (1,)), ((), ()))
bf16 = jnp.bfloat16
f32 = jnp.float32


def local_kernel(
    pick_ref, place_ref, alive_ref, target_ref,
    cot_ref, hid_ref, rid_ref, up_ref, down_ref, w_ref,
    hg_out, gg_out, wg_out, dg_out, ug_out,
    recv_rows, recv_rid, rows, rid, hid, gated_hid, ring, weights, pre,
    w_send, w_recv, maps, part_send, part_recv, part_sum, proj, wide,
    g_send, g_recv, x_send, x_recv, h_send, h_recv,
    gate_part, gate_recv, gate_slots, gate_back,
    in_sem, w_sem, ring_send, ring_recv, hid_sem, p_sem, wg_send, wg_recv,
    gr_sem, x_ssem, x_rsem, hr_sem, gate_sem,
):
    s = lax.axis_index("seq")
    t = lax.axis_index("tp")
    core = s % 2
    chip = s // 2
    z = t // 2
    xl = t % 2
    is_cot = core == xl
    kind = (core + xl) % 2

    def remote(src, dst, ssem, rsem, seq, tp):
        return pltpu.make_async_remote_copy(
            src_ref=src, dst_ref=dst, send_sem=ssem, recv_sem=rsem,
            device_id={"seq": seq, "tp": tp}, device_id_type=pl.DeviceIdType.MESH,
        )

    def wait_bytes(ref, sem):
        pltpu.make_async_copy(ref, ref, sem).wait()

    def load_weights(j, c):
        start = pl.multiple_of((2 * j + core) * WIDTH, WIDTH)
        pltpu.make_async_copy(w_ref.at[pl.ds(start, WIDTH)], weights.at[j], w_sem.at[j]).start()
        return c
    lax.fori_loop(0, RING, load_weights, 0)

    barrier = pltpu.get_barrier_semaphore()

    def greet_seq(i, c):
        pl.semaphore_signal(barrier, inc=1, device_id={"seq": (s + i) % 16, "tp": t},
                            device_id_type=pl.DeviceIdType.MESH)
        return c
    lax.fori_loop(1, 16, greet_seq, 0)

    def greet_tp(i, c):
        for other in range(2):
            pl.semaphore_signal(barrier, inc=1, device_id={"seq": 2 * chip + other, "tp": (t + i) % 16},
                                device_id_type=pl.DeviceIdType.MESH)
        return c
    lax.fori_loop(1, 16, greet_tp, 0)
    pl.semaphore_wait(barrier, 45)

    def give(src, dst, sem_out, sem_in, seq):
        @pl.when(seq == s)
        def _():
            pltpu.make_async_copy(src, dst, sem_in).start()

        @pl.when(seq != s)
        def _():
            remote(src, dst, sem_out, sem_in, seq, t).start()

    my_slots = pl.ds(s * LEVELS, LEVELS)

    def send_first(i, c):
        d = (chip + i) % CHIPS
        give(cot_ref.at[:, d], recv_rows.at[my_slots], in_sem.at[0], in_sem.at[1], 2 * d + xl)
        for other in range(2):
            give(rid_ref.at[:, d], recv_rid.at[my_slots], in_sem.at[2], in_sem.at[3], 2 * d + other)
        return c
    lax.fori_loop(0, CHIPS, send_first, 0)

    def send_second(i, c):
        d = (chip + i) % CHIPS
        give(hid_ref.at[:, d], recv_rows.at[my_slots], in_sem.at[0], in_sem.at[1], 2 * d + 1 - xl)
        return c
    lax.fori_loop(0, CHIPS, send_second, 0)

    def send_maps(i, c):
        d = (chip + i) % CHIPS
        give(up_ref, maps.at[s], in_sem.at[4], in_sem.at[5], 2 * d + xl)
        give(down_ref, maps.at[s], in_sem.at[4], in_sem.at[5], 2 * d + 1 - xl)
        return c
    lax.fori_loop(0, CHIPS, send_maps, 0)

    right = 2 * ((z + 1) % RING) + xl
    left = 2 * ((z + RING - 1) % RING) + xl
    across = 2 * z + 1 - xl
    partner = 2 * chip + 1 - core

    def half(h):
        return pl.ds(h * HALF, HALF)

    def to_right(src, slot, h):
        return remote(src, ring.at[slot, half(h)], ring_send.at[slot, h], ring_recv.at[slot, h], s, right)

    def to_left(src, slot, h):
        return remote(src, ring.at[slot, half(h)], ring_send.at[slot, h], ring_recv.at[slot, h], s, left)

    def to_across(h):
        return remote(ring.at[0, half(h)], ring.at[0, half(h)], ring_send.at[0, h], ring_recv.at[0, h], s, across)

    def to_partner():
        return remote(hid, hid, hid_sem.at[0], hid_sem.at[1], partner, t)

    @pl.when(is_cot)
    def _():
        wait_bytes(recv_rows, in_sem.at[1])

        def pack(g, c):
            value = recv_rows[pick_ref[g]]
            rows[g] = value
            ring[0, g] = value
            return c
        lax.fori_loop(0, GROUPS, pack, 0)
        for h in range(2):
            to_across(h).start()
            to_right(ring.at[0, half(h)], 1, h).start()
            to_left(ring.at[0, half(h)], 2, h).start()

    @pl.when(jnp.logical_not(is_cot))
    def _():
        for h in range(2):
            wait_bytes(ring.at[0, half(h)], ring_recv.at[0, h])
            to_right(ring.at[0, half(h)], 1, h).start()
            to_left(ring.at[0, half(h)], 2, h).start()
        wait_bytes(recv_rows, in_sem.at[1])

        def pack(g, c):
            value = recv_rows[pick_ref[g]]
            rows[g] = value
            hid[g] = value
            return c
        lax.fori_loop(0, GROUPS, pack, 0)
        to_partner().start()

    wait_bytes(recv_rid, in_sem.at[3])

    def pack_rid(g, c):
        rid[g] = recv_rid[pick_ref[g]]
        return c
    lax.fori_loop(0, GROUPS, pack_rid, 0)

    wait_bytes(maps, in_sem.at[5])

    def project(r, c):
        groups = pl.ds(r * GROUP, GROUP)
        x = rows[groups].reshape(RANK, WIDTH)
        y = lax.dot_general(x, maps[...].reshape(NREC * RANK, WIDTH), contract_last, preferred_element_type=f32)
        depth = rid[groups].reshape(RANK, BLOCK)[:, 64:65].astype(f32)
        total = jnp.zeros((RANK, RANK), f32)
        for d in range(NREC):
            total = total + jnp.where(depth == d + 1.0, y[:, d * RANK:(d + 1) * RANK], 0.0)
        part_send[pl.ds(r * RANK, RANK)] = total.astype(bf16)
        return c
    lax.fori_loop(0, ROWS // RANK, project, 0)

    def same_kind(t2):
        return 2 * chip + (core + xl + t2) % 2

    def send_part(i, c):
        t2 = (t + i) % PEERS
        remote(part_send.at[pl.ds(t2 * PART, PART)], part_recv.at[t], p_sem.at[0], p_sem.at[1],
               same_kind(t2), t2).start()
        return c
    lax.fori_loop(1, PEERS, send_part, 0)
    pltpu.make_async_copy(part_send.at[pl.ds(t * PART, PART)], part_recv.at[t], p_sem.at[1]).start()

    @pl.when(is_cot)
    def _():
        wait_bytes(hid, hid_sem.at[1])

    def apply_gate(g, c):
        gate = rid[g][:, 0:1].astype(f32)
        gated_hid[g] = (gate * hid[g].astype(f32)).astype(bf16)
        rows[g] = (gate * rows[g].astype(f32)).astype(bf16)
        return c
    lax.fori_loop(0, GROUPS, apply_gate, 0)
    pre[...] = jnp.zeros_like(pre)

    def step(i, c):
        @pl.when(jnp.logical_and(i % 2 == 1, i < RING - 1))
        def _():
            for h in range(2):
                wait_bytes(ring.at[i, half(h)], ring_recv.at[i, h])

                @pl.when(jnp.logical_or(i < 5, h == 0))
                def _():
                    to_right(ring.at[i, half(h)], i + 2, h).start()
                wait_bytes(ring.at[i + 1, half(h)], ring_recv.at[i + 1, h])

                @pl.when(i < 5)
                def _():
                    to_left(ring.at[i + 1, half(h)], i + 3, h).start()
                if h == 1:
                    @pl.when(i == 5)
                    def _():
                        to_left(ring.at[6, half(h)], 7, h).start()

        @pl.when(i == RING - 1)
        def _():
            for h in range(2):
                wait_bytes(ring.at[RING - 1, half(h)], ring_recv.at[RING - 1, h])

        @pl.when(i == 1)
        def _():
            wait_bytes(part_recv, p_sem.at[1])
            part_sum[...] = jnp.sum(part_recv[...].astype(f32), axis=0).astype(bf16)

            def send_sum(j, c):
                t2 = (t + j) % PEERS
                remote(part_sum, proj.at[t], p_sem.at[2], p_sem.at[3],
                       4 * chip + 1 - same_kind(t2), t2).start()
                return c
            lax.fori_loop(0, PEERS, send_sum, 0)

        @pl.when(i == 3)
        def _():
            wait_bytes(proj, p_sem.at[3])
            flat = proj[...].reshape(ROWS, RANK)
            depth = rid[...].reshape(ROWS, BLOCK)[:, 64:65].astype(f32)
            for d in range(NREC):
                wide[:, d * RANK:(d + 1) * RANK] = jnp.where(
                    depth == d + 1.0, 0.5 * flat.astype(f32), 0.0).astype(bf16)

            @pl.when(jnp.logical_not(is_cot))
            def _():
                def add_adapter(r, c):
                    groups = pl.ds(r * GROUP, GROUP)
                    term = jnp.dot(wide[pl.ds(r * RANK, RANK)], maps[...].reshape(NREC * RANK, WIDTH),
                                   preferred_element_type=f32)
                    pre[groups] = pre[groups] + term.reshape(GROUP, GROUP, WIDTH)
                    return c
                lax.fori_loop(0, ROWS // RANK, add_adapter, 0)

            for q in range(NREC):
                grad = lax.dot_general(wide[:, q * RANK:(q + 1) * RANK], rows[...].reshape(ROWS, WIDTH),
                                       contract_rows, preferred_element_type=f32)
                g_send[q * 4:(q + 1) * 4] = grad.astype(bf16).reshape(4, 64, WIDTH)

            def send_grad(j, c):
                to = (s + j) % 16
                remote(g_send.at[to], g_recv.at[kind, chip], gr_sem.at[0], gr_sem.at[1], to, t).start()
                return c
            lax.fori_loop(1, 16, send_grad, 0)
            pltpu.make_async_copy(g_send.at[s], g_recv.at[kind, chip], gr_sem.at[1]).start()

        shift = jnp.where(i % 2 == 1, 2 * RING - (i + 1) // 2, i // 2)
        origin = (z + shift) % RING
        pltpu.make_async_copy(w_ref.at[pl.ds(0, WIDTH)], weights.at[origin], w_sem.at[origin]).wait()
        block = ring[i].reshape(ROWS, WIDTH)
        pre[...] = pre[...] + jnp.dot(
            block, weights[origin], preferred_element_type=f32).reshape(GROUPS, GROUP, WIDTH)
        w_send[i] = lax.dot_general(
            block, gated_hid[...].reshape(ROWS, WIDTH), contract_rows, preferred_element_type=f32).astype(bf16)
        give(w_send.at[i], w_recv.at[chip], wg_send, wg_recv, 2 * origin + core)
        return c
    lax.fori_loop(0, RING, step, 0)

    ones = jnp.ones((8, WIDTH), bf16)
    for r in range(ROWS // RANK):
        groups = slice(r * GROUP, (r + 1) * GROUP)
        prod = pre[groups].reshape(RANK, WIDTH) * hid[groups].reshape(RANK, WIDTH).astype(f32)
        high = prod.astype(bf16)
        low = (prod - high.astype(f32)).astype(bf16)
        lanes = lax.dot_general(ones, high, contract_last, preferred_element_type=f32)
        lanes = lanes + lax.dot_general(ones, low, contract_last, preferred_element_type=f32)
        gate_part[:, r * RANK:(r + 1) * RANK] = lanes[0:1]
    me = 2 * t + core

    def send_gate(j, c):
        t2 = (t + j) % PEERS
        for other in range(2):
            remote(gate_part, gate_recv.at[me], gate_sem.at[0], gate_sem.at[1], 2 * chip + other, t2).start()
        return c
    lax.fori_loop(1, PEERS, send_gate, 0)
    remote(gate_part, gate_recv.at[me], gate_sem.at[0], gate_sem.at[1], partner, t).start()
    pltpu.make_async_copy(gate_part, gate_recv.at[me], gate_sem.at[1]).start()

    def slot_rows(slot):
        gate = recv_rid[slot][:, 0:1].astype(f32)
        return jnp.where(alive_ref[slot] > 0, gate * pre[place_ref[slot]], 0.0)

    def to_other(d):
        return remote(x_send.at[d], x_recv.at[d], x_ssem.at[d], x_rsem.at[d], partner, t)

    def expand(i, c):
        d = (chip + i) % CHIPS

        def one(j, c):
            x_send[d, j] = slot_rows((2 * d + 1 - core) * LEVELS + j).astype(bf16)
            return c
        lax.fori_loop(0, LEVELS, one, 0)
        to_other(d).start()
        return c
    lax.fori_loop(0, CHIPS, expand, 0)

    def give_back(i, c):
        d = (chip + i) % CHIPS
        wait_bytes(x_recv.at[d], x_rsem.at[d])

        def one(j, c):
            value = slot_rows((2 * d + core) * LEVELS + j) + x_recv[d, j].astype(f32)
            h_send[d, j] = value.astype(bf16)
            return c
        lax.fori_loop(0, LEVELS, one, 0)
        give(h_send.at[d], h_recv.at[chip], hr_sem.at[0], hr_sem.at[1], 2 * d + core)
        return c
    lax.fori_loop(0, CHIPS, give_back, 0)

    wait_bytes(gate_recv, gate_sem.at[1])
    total = jnp.sum(gate_recv[...], axis=0)
    spot = target_ref[core]
    pick = (lax.broadcasted_iota(jnp.int32, (ROWS, CHIPS * BLOCK), 0) == spot).astype(f32).astype(bf16)
    placed = jnp.zeros((8, CHIPS * BLOCK), f32)
    rest = total
    for _ in range(3):
        piece = rest.astype(bf16)
        rest = rest - piece.astype(f32)
        placed = placed + jnp.dot(jnp.broadcast_to(piece, (8, ROWS)), pick, preferred_element_type=f32)
    for d in range(CHIPS):
        gate_slots[d] = placed[0:1, d * BLOCK:(d + 1) * BLOCK]

    def send_slots(i, c):
        d = (chip + i) % CHIPS
        give(gate_slots.at[d], gate_back.at[chip], gate_sem.at[2], gate_sem.at[3], 2 * d + core)
        return c
    lax.fori_loop(0, CHIPS, send_slots, 0)

    wait_bytes(g_recv, gr_sem.at[1])
    ug_out[...] = jnp.sum(g_recv[0].astype(f32), axis=0)
    dg_out[...] = jnp.sum(g_recv[1].astype(f32), axis=0)
    wait_bytes(w_recv, wg_recv)

    def add_up(r, c):
        part = pl.ds(r * 64, 64)
        wg_out[part] = jnp.sum(w_recv[:, part].astype(f32), axis=0)
        return c
    lax.fori_loop(0, 8, add_up, 0)
    wait_bytes(h_recv, hr_sem.at[1])
    for d in range(CHIPS):
        hg_out[:, d] = h_recv[d].astype(f32)
    wait_bytes(gate_back, gate_sem.at[3])
    gg_out[...] = gate_back[...]

    wait_bytes(recv_rows.at[pl.ds(0, 15 * LEVELS)], in_sem.at[0])
    wait_bytes(recv_rid.at[pl.ds(0, 15 * LEVELS)], in_sem.at[2])
    wait_bytes(maps.at[pl.ds(0, 15)], in_sem.at[4])

    @pl.when(is_cot)
    def _():
        for h in range(2):
            to_across(h).wait_send()

    @pl.when(jnp.logical_not(is_cot))
    def _():
        to_partner().wait_send()
    for h in range(2):
        for slot in range(1, 7):
            to_right(ring.at[slot, half(h)], slot, h).wait_send()
        to_right(ring.at[7, half(h)], 7, h).wait_send()
    wait_bytes(part_recv.at[pl.ds(0, 15)], p_sem.at[0])
    wait_bytes(proj, p_sem.at[2])
    wait_bytes(g_send.at[pl.ds(0, 15)], gr_sem.at[0])
    wait_bytes(w_send.at[pl.ds(0, 7)], wg_send)
    for d in range(CHIPS):
        to_other(d).wait_send()
    wait_bytes(h_send.at[pl.ds(0, 7)], hr_sem.at[0])
    wait_bytes(gate_recv.at[pl.ds(0, 31)], gate_sem.at[0])
    wait_bytes(gate_slots.at[pl.ds(0, 7)], gate_sem.at[2])


def local(hidden, cotangent, router_gate, recursion_depth, live_counts, out_weight, adapter_down, adapter_up):
    blocks = live_counts // BLOCK
    finish = jnp.cumsum(blocks)
    begin = finish - blocks
    level = jnp.arange(LEVELS, dtype=jnp.int32)
    alive = level[None, :] < blocks[:, None]
    place = jnp.where(alive, begin[:, None] + level[None, :], 0)
    order = jnp.arange(GROUPS, dtype=jnp.int32)
    source = jnp.sum((finish[None, :] <= order[:, None]).astype(jnp.int32), axis=1)
    shard = jnp.arange(16, dtype=jnp.int32)
    first = jnp.sum(jnp.where(source[:, None] == shard[None, :], begin[None, :], 0), axis=1)
    pick = source * LEVELS + order - first
    inside = jnp.arange(GROUP, dtype=jnp.int32)
    target = jnp.where(alive[:, :, None], place[:, :, None] * GROUP + inside, -1)
    target = target.reshape(CHIPS, 2, LEVELS * GROUP).transpose(1, 0, 2)
    target = jnp.pad(target, ((0, 0), (0, 0), (0, BLOCK - LEVELS * GROUP)), constant_values=-1)
    target = target.reshape(2, 1, CHIPS * BLOCK).astype(jnp.int32)
    rider = jnp.where(
        jnp.arange(BLOCK)[None, :] < 64, router_gate[:, None], recursion_depth[:, None].astype(bf16)
    ).astype(bf16).reshape(LEVELS, CHIPS, GROUP, BLOCK)
    split = (LEVELS, CHIPS, GROUP, WIDTH)
    smem = pl.BlockSpec(memory_space=pltpu.SMEM)
    vmem = pl.BlockSpec(memory_space=pltpu.VMEM)
    out = pl.pallas_call(
        local_kernel,
        out_shape=(
            jax.ShapeDtypeStruct(split, f32),
            jax.ShapeDtypeStruct((CHIPS, 1, BLOCK), f32),
            jax.ShapeDtypeStruct((WIDTH, WIDTH), f32),
            jax.ShapeDtypeStruct((64, WIDTH), f32),
            jax.ShapeDtypeStruct((64, WIDTH), f32),
        ),
        in_specs=[smem, smem, smem, vmem, vmem, vmem, vmem, vmem, vmem, pl.BlockSpec(memory_space=pl.ANY)],
        out_specs=(vmem,) * 5,
        scratch_shapes=[
            pltpu.VMEM((96, GROUP, WIDTH), bf16),
            pltpu.VMEM((96, GROUP, BLOCK), bf16),
            pltpu.VMEM((GROUPS, GROUP, WIDTH), bf16),
            pltpu.VMEM((GROUPS, GROUP, BLOCK), bf16),
            pltpu.VMEM((GROUPS, GROUP, WIDTH), bf16),
            pltpu.VMEM((GROUPS, GROUP, WIDTH), bf16),
            pltpu.VMEM((RING, GROUPS, GROUP, WIDTH), bf16),
            pltpu.VMEM((RING, WIDTH, WIDTH), bf16),
            pltpu.VMEM((GROUPS, GROUP, WIDTH), f32),
            pltpu.VMEM((RING, WIDTH, WIDTH), bf16),
            pltpu.VMEM((CHIPS, WIDTH, WIDTH), bf16),
            pltpu.VMEM((16, 64, WIDTH), bf16),
            pltpu.VMEM((ROWS, RANK), bf16),
            pltpu.VMEM((PEERS, PART, RANK), bf16),
            pltpu.VMEM((PART, RANK), bf16),
            pltpu.VMEM((PEERS, PART, RANK), bf16),
            pltpu.VMEM((ROWS, NREC * RANK), bf16),
            pltpu.VMEM((16, 64, WIDTH), bf16),
            pltpu.VMEM((2, CHIPS, 64, WIDTH), bf16),
            pltpu.VMEM((CHIPS, LEVELS, GROUP, WIDTH), bf16),
            pltpu.VMEM((CHIPS, LEVELS, GROUP, WIDTH), bf16),
            pltpu.VMEM((CHIPS, LEVELS, GROUP, WIDTH), bf16),
            pltpu.VMEM((CHIPS, LEVELS, GROUP, WIDTH), bf16),
            pltpu.VMEM((1, ROWS), f32),
            pltpu.VMEM((32, 1, ROWS), f32),
            pltpu.VMEM((CHIPS, 1, BLOCK), f32),
            pltpu.VMEM((CHIPS, 1, BLOCK), f32),
            pltpu.SemaphoreType.DMA((6,)),
            pltpu.SemaphoreType.DMA((RING,)),
            pltpu.SemaphoreType.DMA((RING, 2)),
            pltpu.SemaphoreType.DMA((RING, 2)),
            pltpu.SemaphoreType.DMA((2,)),
            pltpu.SemaphoreType.DMA((4,)),
            pltpu.SemaphoreType.DMA,
            pltpu.SemaphoreType.DMA,
            pltpu.SemaphoreType.DMA((2,)),
            pltpu.SemaphoreType.DMA((CHIPS,)),
            pltpu.SemaphoreType.DMA((CHIPS,)),
            pltpu.SemaphoreType.DMA((2,)),
            pltpu.SemaphoreType.DMA((4,)),
        ],
        compiler_params=pltpu.CompilerParams(
            collective_id=0, has_side_effects=True, vmem_limit_bytes=VMEM_LIMIT
        ),
    )(
        pick, place.reshape(96), alive.reshape(96).astype(jnp.int32), target,
        cotangent.reshape(split), hidden.reshape(split), rider,
        adapter_up, adapter_down.T, out_weight,
    )
    hidden_grad, gate_back, weight_grad, down_grad, up_grad = out
    gate_grad = gate_back[:, 0, : LEVELS * GROUP].reshape(CHIPS, LEVELS, GROUP).transpose(1, 0, 2).reshape(-1)
    return hidden_grad.reshape(hidden.shape), gate_grad, weight_grad, down_grad, up_grad


def solution(mesh):
    in_specs = (
        P("seq", "tp"),
        P("seq", "tp"),
        P("seq"),
        P("seq"),
        P(),
        P(None, "tp"),
        P("tp", "seq"),
        P("seq", "tp"),
    )
    out_specs = (P("seq", "tp"), P("seq"), P("seq", "tp"), P("seq", "tp"), P("seq", "tp"))
    return jax.shard_map(local, mesh=mesh, in_specs=in_specs, out_specs=out_specs, check_vma=False)
```

time: 744 us -> 202 us (0.27)
  the two profiles are of different devices: /device:TPU:4 before, /device:TPU:162 now
where the time goes in v1:
time: 202 us
  Pallas kernels  187 us (93%)
  local copies, waits for them, and re-layouts  9.69 us (5%)
  other arithmetic  4.65 us (2%)
    pallas_call x1, Pallas kernels, local(): pl.pallas_call(local_kernel, out_shape=(jax.ShapeDtypeStruct(split, f32),...  187 us
    unnamed x11, local copies, waits for them, and re-layouts  5.07 us

profile of v1, /device:TPU:162, one launch (start us, length us, event | category | flops | bytes accessed | tf_op | source)
XLA Modules:
  0.0 201.9 jit_solution(9888189926045324644)
XLA Ops:
  0.6 0.7 and_select_fusion
  1.3 0.7 fusion.2
  2.0 0.7 convert_element_type.15
  2.7 0.1 add.49
  2.7 0.1 copy.17
  2.9 0.1 reduce
  3.0 0.7 fusion.1
  3.6 0.1 convert_reduce_fusion
  3.7 0.1 select_reduce_fusion
  3.8 0.5 add_subtract_fusion.pick_ref
  4.3 0.1 broadcast_in_dim.82
  4.4 0.1 iota_compare_fusion
  4.5 0.6 reshape.159.alive_ref
  5.1 0.8 broadcast_in_dim.80
  5.9 0.1 broadcast_in_dim.76
  6.0 0.1 broadcast_in_dim.77
  6.1 0.1 broadcast_multiply_fusion
  6.1 0.6 select_n.34.place_ref
  6.7 0.1 add.46
  6.8 0.1 add.47
  6.9 0.6 pad.4.clone
  7.6 0.9 broadcast_select_fusion.rid_ref
  8.5 186.9 %shard_map.119 = (f32[6,8,16,512]{3,2,1,0:T(8,128)}, f32[8,1,128]{2,1,0:T(1,128)}, f32[512,512]{1,0:T(8,128)}, f32[64,512]{1,0:T(8,128)}, f32[64,512]{1,0:T(8,128)}) custom-call(s32[48]{0:T(128)} %add_subtract_fusion.pick_ref, s32[96]{0:T(128)} %select_n.34.place_ref, s32[96]{0:T(128)} %reshape.159.alive_ref, s32[2,1,1024]{2,1,0:T(1,128)} %bitcast.15, ...), custom_call_target="tpu_custom_call" | custom-call | tf_op jit(solution)/shard_map/pallas_call | solution.py:422
  195.4 0.7 slice_reduce_fusion
  196.1 0.1 reshape_squeeze.3
  196.2 0.7 reshape.158
  196.8 0.0 copy-start
  196.8 2.8 %copy.25 = f32[768,512]{1,0:T(8,128)} copy(f32[768,512]{1,0:T(8,128)} %bitcast.10) | data formatting | bytes 3145728
  199.6 0.0 copy-done
  199.6 0.0 copy-start.2
  199.6 0.0 copy-start.1
  199.6 1.0 copy.26
  200.6 0.0 copy-done.2
  200.6 0.7 copy.27
  201.2 0.0 copy-done.1
  201.2 0.7 copy.28
  (6 shorter events, 0.1 us)
Async XLA Ops:
  196.8 2.8 %copy-start = (f32[512,512]{1,0:T(8,128)S(1)}, f32[512,512]{1,0:T(8,128)}, u32[]{:S(2)}) copy-start(f32[512,512]{1,0:T(8,128)} %get-tuple-element.26) | copy-start | bytes 3145732
  199.6 1.0 copy-start.2
  199.6 1.7 copy-start.1

commit v2 on v1

v2 whole, which is shorter than its diff:
```python
import functools

import jax
import jax.numpy as jnp
from jax import lax
from jax.experimental import pallas as pl
from jax.experimental.pallas import tpu as pltpu
from jax.sharding import PartitionSpec as P

NREC = 4
BLOCK = 128
GROUP = 16
CHIPS = 8
LEVELS = 6
GROUPS = 48
ROWS = GROUPS * GROUP
RING = 8
WIDTH = 512
HALF = WIDTH // 2
RANK = 256
PART = 48
PEERS = 16
PIECE = 64
VMEM_LIMIT = 60 * 1024 * 1024

contract_rows = (((0,), (0,)), ((), ()))
contract_last = (((1,), (1,)), ((), ()))
bf16 = jnp.bfloat16
f32 = jnp.float32


def local_kernel(
    pick, place, alive, cot_ref, hid_ref, rid_ref, up_ref, down_ref, w_ref,
    hg_out, gg_out, wg_out, dg_out, ug_out,
    recv_low, recv_high, recv_rid, slot_gate, slot_depth, gates, depths,
    rows, hid, gated_hid, ring, weights, pre,
    w_send, w_recv, sum_send, sum_recv, maps, part_send, part_recv, part_sum, proj, wide,
    g_send, g_recv, x_send, x_recv, h_send, h_recv,
    gate_part, gate_recv, gate_rows, gate_slots, gate_back,
    in_sem, w_sem, ring_send, ring_recv, hid_sem, p_sem, wg_send, wg_recv, sum_sem,
    gr_sem, x_ssem, x_rsem, hr_sem, gate_sem,
):
    s = lax.axis_index("seq")
    t = lax.axis_index("tp")
    core = s % 2
    chip = s // 2
    z = t // 2
    xl = t % 2
    is_cot = core == xl
    kind = (core + xl) % 2
    recv_rows = (recv_low, recv_high)

    def remote(src, dst, ssem, rsem, seq, tp):
        return pltpu.make_async_remote_copy(
            src_ref=src, dst_ref=dst, send_sem=ssem, recv_sem=rsem,
            device_id={"seq": seq, "tp": tp}, device_id_type=pl.DeviceIdType.MESH,
        )

    def wait_bytes(ref, sem):
        pltpu.make_async_copy(ref, ref, sem).wait()

    barrier = pltpu.get_barrier_semaphore()

    def greet_tp(i, c):
        for other in range(2):
            pl.semaphore_signal(barrier, inc=1, device_id={"seq": 2 * chip + other, "tp": (t + i) % 16},
                                device_id_type=pl.DeviceIdType.MESH)
        return c
    lax.fori_loop(1, 16, greet_tp, 0)

    def greet_seq(i, c):
        pl.semaphore_signal(barrier, inc=1, device_id={"seq": (s + i) % 16, "tp": t},
                            device_id_type=pl.DeviceIdType.MESH)
        return c
    lax.fori_loop(1, 16, greet_seq, 0)

    def load_weights(j, c):
        pltpu.make_async_copy(w_ref.at[2 * j + core], weights.at[j], w_sem.at[j]).start()
        return c
    lax.fori_loop(0, RING, load_weights, 0)
    pl.semaphore_wait(barrier, 45)

    def give(src, dst, sem_out, sem_in, seq):
        @pl.when(seq == s)
        def _():
            pltpu.make_async_copy(src, dst, sem_in).start()

        @pl.when(seq != s)
        def _():
            remote(src, dst, sem_out, sem_in, seq, t).start()

    my_slots = pl.ds(s * LEVELS, LEVELS)

    def half(h):
        return pl.ds(h * HALF, HALF)

    def send_first(h, i, c):
        d = (chip + i) % CHIPS
        give(cot_ref.at[:, d, :, half(h)], recv_rows[h].at[my_slots], in_sem.at[h], in_sem.at[6 + h], 2 * d + xl)
        return c
    for h in range(2):
        lax.fori_loop(0, CHIPS, functools.partial(send_first, h), 0)

    def send_rid(i, c):
        d = (chip + i) % CHIPS
        for other in range(2):
            give(rid_ref, recv_rid.at[s], in_sem.at[2], in_sem.at[3], 2 * d + other)
        return c
    lax.fori_loop(0, CHIPS, send_rid, 0)

    def send_second():
        def send_hid(i, c):
            d = (chip + i) % CHIPS
            for h in range(2):
                give(hid_ref.at[:, d, :, half(h)], recv_rows[h].at[my_slots], in_sem.at[h], in_sem.at[6 + h],
                     2 * d + 1 - xl)
            return c
        lax.fori_loop(0, CHIPS, send_hid, 0)

        def send_maps(i, c):
            d = (chip + i) % CHIPS
            give(up_ref, maps.at[s], in_sem.at[4], in_sem.at[5], 2 * d + xl)
            give(down_ref, maps.at[s], in_sem.at[4], in_sem.at[5], 2 * d + 1 - xl)
            return c
        lax.fori_loop(0, CHIPS, send_maps, 0)

    right = 2 * ((z + 1) % RING) + xl
    left = 2 * ((z + RING - 1) % RING) + xl
    across = 2 * z + 1 - xl
    partner = 2 * chip + 1 - core

    def to_right(src, slot, h):
        return remote(src, ring.at[slot, h], ring_send.at[slot, h], ring_recv.at[slot, h], s, right)

    def to_left(src, slot, h):
        return remote(src, ring.at[slot, h], ring_send.at[slot, h], ring_recv.at[slot, h], s, left)

    def to_across(h):
        return remote(ring.at[0, h], ring.at[0, h], ring_send.at[0, h], ring_recv.at[0, h], s, across)

    def to_partner():
        return remote(hid, hid, hid_sem.at[0], hid_sem.at[1], partner, t)

    def forward(i):
        for h in range(2):
            wait_bytes(ring.at[i, h], ring_recv.at[i, h])
            if i < 5 or h == 0:
                to_right(ring.at[i, h], i + 2, h).start()
            wait_bytes(ring.at[i + 1, h], ring_recv.at[i + 1, h])
            if i < 5:
                to_left(ring.at[i + 1, h], i + 3, h).start()
            elif h == 1:
                to_left(ring.at[6, h], 7, h).start()

    @pl.when(is_cot)
    def _():
        for h in range(2):
            wait_bytes(recv_rows[h], in_sem.at[6 + h])

            def pack(g, c):
                value = recv_rows[h][pick[g]]
                rows[g, :, h * HALF:(h + 1) * HALF] = value
                ring[0, h, g] = value
                return c
            lax.fori_loop(0, GROUPS, pack, 0, unroll=4)
            to_across(h).start()
            to_right(ring.at[0, h], 1, h).start()
            to_left(ring.at[0, h], 2, h).start()

    @pl.when(jnp.logical_not(is_cot))
    def _():
        for h in range(2):
            wait_bytes(ring.at[0, h], ring_recv.at[0, h])
            to_right(ring.at[0, h], 1, h).start()
            to_left(ring.at[0, h], 2, h).start()
    send_second()

    wait_bytes(recv_rid, in_sem.at[3])
    lane = lax.broadcasted_iota(jnp.int32, (GROUP, BLOCK), 1)
    row = lax.broadcasted_iota(jnp.int32, (GROUP, BLOCK), 0)
    chosen = (lane == chip * GROUP + row).astype(f32).astype(bf16)
    columns = lax.dot_general(chosen, recv_rid[...].reshape(16 * GROUP, BLOCK).astype(bf16), contract_last,
                              preferred_element_type=f32)
    for i in range(16):
        for j in range(LEVELS):
            at = i * GROUP + j
            slot_gate[i * LEVELS + j] = jnp.broadcast_to(columns[:, at:at + 1], (GROUP, BLOCK))
            slot_depth[i * LEVELS + j] = jnp.broadcast_to(columns[:, at + 8:at + 9], (GROUP, BLOCK))

    def pack_rid(g, c):
        gates[g] = slot_gate[pick[g]]
        depths[g] = slot_depth[pick[g]]
        return c
    lax.fori_loop(0, GROUPS, pack_rid, 0, unroll=4)
    pre[...] = jnp.zeros_like(pre)

    forward(1)

    @pl.when(jnp.logical_not(is_cot))
    def _():
        for h in range(2):
            wait_bytes(recv_rows[h], in_sem.at[6 + h])

            def pack(g, c):
                value = recv_rows[h][pick[g]]
                rows[g, :, h * HALF:(h + 1) * HALF] = value
                hid[g, :, h * HALF:(h + 1) * HALF] = value
                return c
            lax.fori_loop(0, GROUPS, pack, 0, unroll=4)
        to_partner().start()

    wait_bytes(maps, in_sem.at[5])

    def project(r, c):
        groups = pl.ds(r * GROUP, GROUP)
        x = rows[groups].reshape(RANK, WIDTH)
        y = lax.dot_general(x, maps[...].reshape(NREC * RANK, WIDTH), contract_last, preferred_element_type=f32)
        depth = depths[groups].reshape(RANK, BLOCK)[:, 0:1]
        total = jnp.zeros((RANK, RANK), f32)
        for d in range(NREC):
            total = total + jnp.where(depth == d + 1.0, y[:, d * RANK:(d + 1) * RANK], 0.0)
        part_send[pl.ds(r * RANK, RANK)] = total.astype(bf16)
        return c
    lax.fori_loop(0, ROWS // RANK, project, 0)

    def same_kind(t2):
        return 2 * chip + (core + xl + t2) % 2

    def send_part(i, c):
        t2 = (t + i) % PEERS
        remote(part_send.at[pl.ds(t2 * PART, PART)], part_recv.at[t], p_sem.at[0], p_sem.at[1],
               same_kind(t2), t2).start()
        return c
    lax.fori_loop(1, PEERS, send_part, 0)
    pltpu.make_async_copy(part_send.at[pl.ds(t * PART, PART)], part_recv.at[t], p_sem.at[1]).start()

    @pl.when(is_cot)
    def _():
        wait_bytes(hid, hid_sem.at[1])

    def apply_gate(g, c):
        gate = gates[g][:, 0:1]
        gated_hid[g] = (gate * hid[g].astype(f32)).astype(bf16)
        rows[g] = (gate * rows[g].astype(f32)).astype(bf16)
        return c
    lax.fori_loop(0, GROUPS, apply_gate, 0, unroll=4)

    def origin_of(i):
        shift = jnp.where(i % 2 == 1, 2 * RING - (i + 1) // 2, i // 2)
        return (z + shift) % RING

    def compute(i, c):
        origin = origin_of(i)
        pltpu.make_async_copy(w_ref.at[0], weights.at[origin], w_sem.at[origin]).wait()
        for h in range(2):
            w_send[i, h * 4:(h + 1) * 4] = lax.dot_general(
                ring[i, h].reshape(ROWS, HALF), gated_hid[...].reshape(ROWS, WIDTH), contract_rows,
                preferred_element_type=f32).astype(bf16).reshape(4, PIECE, WIDTH)

        give(w_send.at[i], w_recv.at[chip], wg_send, wg_recv.at[0], 2 * origin + core)
        term = jnp.dot(ring[i, 0].reshape(ROWS, HALF), weights[origin, 0], preferred_element_type=f32)
        term = term + jnp.dot(ring[i, 1].reshape(ROWS, HALF), weights[origin, 1], preferred_element_type=f32)
        pre[...] = pre[...] + term.reshape(GROUPS, GROUP, WIDTH)
        return c

    def run(i, c):
        @pl.when(i == 3)
        def _():
            forward(3)
            wait_bytes(part_recv, p_sem.at[1])
            part_sum[...] = jnp.sum(part_recv[...].astype(f32), axis=0).astype(bf16)

            def send_sum(j, c):
                t2 = (t + j) % PEERS
                remote(part_sum, proj.at[t], p_sem.at[2], p_sem.at[3],
                       4 * chip + 1 - same_kind(t2), t2).start()
                return c
            lax.fori_loop(0, PEERS, send_sum, 0)

        @pl.when(i == 5)
        def _():
            forward(5)

        @pl.when(i == RING - 1)
        def _():
            wait_bytes(proj, p_sem.at[3])
            flat = proj[...].reshape(ROWS, RANK)
            depth = depths[...].reshape(ROWS, BLOCK)[:, 0:1]
            for d in range(NREC):
                wide[:, d * RANK:(d + 1) * RANK] = jnp.where(
                    depth == d + 1.0, 0.5 * flat.astype(f32), 0.0).astype(bf16)

            @pl.when(jnp.logical_not(is_cot))
            def _():
                def add_adapter(r, c):
                    groups = pl.ds(r * GROUP, GROUP)
                    term = jnp.dot(wide[pl.ds(r * RANK, RANK)], maps[...].reshape(NREC * RANK, WIDTH),
                                   preferred_element_type=f32)
                    pre[groups] = pre[groups] + term.reshape(GROUP, GROUP, WIDTH)
                    return c
                lax.fori_loop(0, ROWS // RANK, add_adapter, 0)

            for q in range(NREC):
                grad = lax.dot_general(wide[:, q * RANK:(q + 1) * RANK], rows[...].reshape(ROWS, WIDTH),
                                       contract_rows, preferred_element_type=f32)
                g_send[q * 4:(q + 1) * 4] = grad.astype(bf16).reshape(4, PIECE, WIDTH)

            def send_grad(j, c):
                to = (s + j) % 16
                remote(g_send.at[to], g_recv.at[kind, chip], gr_sem.at[0], gr_sem.at[1], to, t).start()
                return c
            lax.fori_loop(1, 16, send_grad, 0)
            pltpu.make_async_copy(g_send.at[s], g_recv.at[kind, chip], gr_sem.at[1]).start()
            for h in range(2):
                wait_bytes(ring.at[RING - 1, h], ring_recv.at[RING - 1, h])

        compute(i, c)
        return c
    lax.fori_loop(0, RING, run, 0)

    ones = jnp.ones((8, WIDTH), bf16)
    for r in range(ROWS // RANK):
        groups = slice(r * GROUP, (r + 1) * GROUP)
        prod = pre[groups].reshape(RANK, WIDTH) * hid[groups].reshape(RANK, WIDTH).astype(f32)
        high = prod.astype(bf16)
        low = (prod - high.astype(f32)).astype(bf16)
        lanes = lax.dot_general(ones, high, contract_last, preferred_element_type=f32)
        lanes = lanes + lax.dot_general(ones, low, contract_last, preferred_element_type=f32)
        gate_part[:, r * RANK:(r + 1) * RANK] = lanes[0:1]
    me = 2 * t + core

    def send_gate(j, c):
        t2 = (t + j) % PEERS
        for other in range(2):
            remote(gate_part, gate_recv.at[me], gate_sem.at[0], gate_sem.at[1], 2 * chip + other, t2).start()
        return c
    lax.fori_loop(1, PEERS, send_gate, 0)
    remote(gate_part, gate_recv.at[me], gate_sem.at[0], gate_sem.at[1], partner, t).start()
    pltpu.make_async_copy(gate_part, gate_recv.at[me], gate_sem.at[1]).start()

    def slot_rows(slot):
        gate = slot_gate[slot][:, 0:1]
        return jnp.where(alive[slot] > 0, gate * pre[place[slot]], 0.0)

    def to_other(d):
        return remote(x_send.at[d], x_recv.at[d], x_ssem.at[d], x_rsem.at[d], partner, t)

    def expand(i, c):
        d = (chip + i) % CHIPS
        for j in range(LEVELS):
            x_send[d, j] = slot_rows((2 * d + 1 - core) * LEVELS + j).astype(bf16)
        to_other(d).start()
        return c
    lax.fori_loop(0, CHIPS, expand, 0)

    def give_back(i, c):
        d = (chip + i) % CHIPS
        wait_bytes(x_recv.at[d], x_rsem.at[d])
        for j in range(LEVELS):
            value = slot_rows((2 * d + core) * LEVELS + j) + x_recv[d, j].astype(f32)
            h_send[d, j] = value.astype(bf16)
        give(h_send.at[d], h_recv.at[chip], hr_sem.at[0], hr_sem.at[1], 2 * d + core)
        return c
    lax.fori_loop(0, CHIPS, give_back, 0)

    wait_bytes(gate_recv, gate_sem.at[1])
    total = jnp.sum(gate_recv[...], axis=0)
    group_of = lax.shift_right_logical(lax.broadcasted_iota(jnp.int32, (GROUPS, ROWS), 1), 4)
    rest = jnp.where(group_of == lax.broadcasted_iota(jnp.int32, (GROUPS, ROWS), 0), total, 0.0)
    low_bits = jnp.bitwise_and(lax.broadcasted_iota(jnp.int32, (ROWS, BLOCK), 0), GROUP - 1)
    low_lane = jnp.bitwise_and(lax.broadcasted_iota(jnp.int32, (ROWS, BLOCK), 1), GROUP - 1)
    fold = (low_bits == low_lane).astype(f32).astype(bf16)
    folded = jnp.zeros((GROUPS, BLOCK), f32)
    for _ in range(3):
        piece = rest.astype(bf16)
        rest = rest - piece.astype(f32)
        folded = folded + jnp.dot(piece, fold, preferred_element_type=f32)
    for g in range(GROUPS):
        gate_rows[g] = folded[g:g + 1]
    mine = lax.shift_right_logical(lax.broadcasted_iota(jnp.int32, (1, BLOCK), 1), 4) == chip

    for d in range(CHIPS):
        lines = []
        for j in range(LEVELS):
            slot = (2 * d + core) * LEVELS + j
            value = jnp.where(alive[slot] > 0, gate_rows[place[slot]], 0.0)
            lines.append(jnp.where(mine, value, 0.0))
        gate_slots[d] = jnp.concatenate(lines + [jnp.zeros((2, BLOCK), f32)], axis=0)

    def give_slots(i, c):
        d = (chip + i) % CHIPS
        give(gate_slots.at[d], gate_back.at[chip], gate_sem.at[2], gate_sem.at[3], 2 * d + core)
        return c
    lax.fori_loop(0, CHIPS, give_slots, 0)

    wait_bytes(g_recv, gr_sem.at[1])
    ug_out[...] = jnp.sum(g_recv[0].astype(f32), axis=0)
    dg_out[...] = jnp.sum(g_recv[1].astype(f32), axis=0)
    wait_bytes(h_recv, hr_sem.at[1])
    hg_out[...] = h_recv[...]
    wait_bytes(w_recv, wg_recv.at[0])
    for d in range(CHIPS):
        wg_out[d * PIECE:(d + 1) * PIECE] = jnp.sum(w_recv[:, d].astype(f32), axis=0)
    wait_bytes(gate_back, gate_sem.at[3])
    gg_out[...] = jnp.sum(gate_back[...], axis=0)

    for h in range(2):
        wait_bytes(recv_rows[h].at[pl.ds(0, 15 * LEVELS)], in_sem.at[h])
    wait_bytes(recv_rid.at[pl.ds(0, 15)], in_sem.at[2])
    wait_bytes(maps.at[pl.ds(0, 15)], in_sem.at[4])

    @pl.when(is_cot)
    def _():
        for h in range(2):
            to_across(h).wait_send()

    @pl.when(jnp.logical_not(is_cot))
    def _():
        to_partner().wait_send()
    for h in range(2):
        for slot in range(1, 7):
            to_right(ring.at[slot, h], slot, h).wait_send()
        to_right(ring.at[7, h], 7, h).wait_send()
    wait_bytes(part_recv.at[pl.ds(0, 15)], p_sem.at[0])
    wait_bytes(proj, p_sem.at[2])
    wait_bytes(g_send.at[pl.ds(0, 15)], gr_sem.at[0])
    wait_bytes(w_send.at[pl.ds(0, 7)], wg_send)
    for d in range(CHIPS):
        to_other(d).wait_send()
    wait_bytes(h_send.at[pl.ds(0, 7)], hr_sem.at[0])
    wait_bytes(gate_recv.at[pl.ds(0, 31)], gate_sem.at[0])
    wait_bytes(gate_slots.at[pl.ds(0, 7)], gate_sem.at[2])


def local(hidden, cotangent, router_gate, recursion_depth, live_counts, out_weight, adapter_down, adapter_up):
    rider = jnp.stack([router_gate.astype(f32), recursion_depth.astype(f32)]).reshape(2, LEVELS, BLOCK)
    rider = jnp.pad(rider, ((0, 0), (0, 2), (0, 0))).reshape(16, BLOCK)
    split = (LEVELS, CHIPS, GROUP, WIDTH)
    blocks = live_counts // BLOCK
    finish = jnp.cumsum(blocks)
    begin = finish - blocks
    level = jnp.arange(LEVELS, dtype=jnp.int32)
    alive = level[None, :] < blocks[:, None]
    place = jnp.where(alive, begin[:, None] + level[None, :], 0)
    order = jnp.arange(GROUPS, dtype=jnp.int32)
    past = finish[None, :] <= order[:, None]
    source = jnp.sum(past.astype(jnp.int32), axis=1)
    first = jnp.max(jnp.where(past, finish[None, :], 0), axis=1)
    pick = source * LEVELS + order - first
    vmem = pl.BlockSpec(memory_space=pltpu.VMEM)
    grouped = (GROUPS, GROUP, WIDTH)
    slots = (CHIPS, LEVELS, GROUP, WIDTH)
    dma = pltpu.SemaphoreType.DMA
    out = pl.pallas_call(
        local_kernel,
        out_shape=(
            jax.ShapeDtypeStruct(slots, bf16),
            jax.ShapeDtypeStruct((8, BLOCK), f32),
            jax.ShapeDtypeStruct((WIDTH, WIDTH), f32),
            jax.ShapeDtypeStruct((PIECE, WIDTH), f32),
            jax.ShapeDtypeStruct((PIECE, WIDTH), f32),
        ),
        in_specs=[pl.BlockSpec(memory_space=pltpu.SMEM)] * 3 + [vmem] * 5 + [pl.BlockSpec(memory_space=pl.ANY)],
        out_specs=(vmem,) * 5,
        scratch_shapes=[
            pltpu.VMEM((96, GROUP, HALF), bf16),
            pltpu.VMEM((96, GROUP, HALF), bf16),
            pltpu.VMEM((16, 16, BLOCK), f32),
            pltpu.VMEM((96, GROUP, BLOCK), f32),
            pltpu.VMEM((96, GROUP, BLOCK), f32),
            pltpu.VMEM((GROUPS, GROUP, BLOCK), f32),
            pltpu.VMEM((GROUPS, GROUP, BLOCK), f32),
            pltpu.VMEM(grouped, bf16),
            pltpu.VMEM(grouped, bf16),
            pltpu.VMEM(grouped, bf16),
            pltpu.VMEM((RING, 2, GROUPS, GROUP, HALF), bf16),
            pltpu.VMEM((RING, 2, HALF, WIDTH), bf16),
            pltpu.VMEM(grouped, f32),
            pltpu.VMEM((RING, CHIPS, PIECE, WIDTH), bf16),
            pltpu.VMEM((RING, CHIPS, PIECE, WIDTH), bf16),
            pltpu.VMEM((RING, PIECE, WIDTH), bf16),
            pltpu.VMEM((CHIPS, PIECE, WIDTH), bf16),
            pltpu.VMEM((16, PIECE, WIDTH), bf16),
            pltpu.VMEM((ROWS, RANK), bf16),
            pltpu.VMEM((PEERS, PART, RANK), bf16),
            pltpu.VMEM((PART, RANK), bf16),
            pltpu.VMEM((PEERS, PART, RANK), bf16),
            pltpu.VMEM((ROWS, NREC * RANK), bf16),
            pltpu.VMEM((16, PIECE, WIDTH), bf16),
            pltpu.VMEM((2, CHIPS, PIECE, WIDTH), bf16),
            pltpu.VMEM(slots, bf16),
            pltpu.VMEM(slots, bf16),
            pltpu.VMEM(slots, bf16),
            pltpu.VMEM(slots, bf16),
            pltpu.VMEM((1, ROWS), f32),
            pltpu.VMEM((32, 1, ROWS), f32),
            pltpu.VMEM((GROUPS, 1, BLOCK), f32),
            pltpu.VMEM((CHIPS, 8, BLOCK), f32),
            pltpu.VMEM((CHIPS, 8, BLOCK), f32),
            dma((8,)),
            dma((RING,)),
            dma((RING, 2)),
            dma((RING, 2)),
            dma((2,)),
            dma((4,)),
            dma,
            dma((RING,)),
            dma((2,)),
            dma((2,)),
            dma((CHIPS,)),
            dma((CHIPS,)),
            dma((2,)),
            dma((4,)),
        ],
        compiler_params=pltpu.CompilerParams(
            collective_id=0, has_side_effects=True, vmem_limit_bytes=VMEM_LIMIT
        ),
    )(
        pick, place.reshape(96), alive.reshape(96).astype(jnp.int32), cotangent.reshape(split), hidden.reshape(split), rider,
        adapter_up, adapter_down.T, out_weight.reshape(PEERS, 2, HALF, WIDTH),
    )
    hidden_grad, gate_back, weight_grad, down_grad, up_grad = out
    hidden_grad = hidden_grad.transpose(1, 0, 2, 3).reshape(hidden.shape).astype(f32)
    return hidden_grad, gate_back[:LEVELS].reshape(-1), weight_grad, down_grad, up_grad


def solution(mesh):
    in_specs = (
        P("seq", "tp"),
        P("seq", "tp"),
        P("seq"),
        P("seq"),
        P(),
        P(None, "tp"),
        P("tp", "seq"),
        P("seq", "tp"),
    )
    out_specs = (P("seq", "tp"), P("seq"), P("seq", "tp"), P("seq", "tp"), P("seq", "tp"))
    return jax.shard_map(local, mesh=mesh, in_specs=in_specs, out_specs=out_specs, check_vma=False)
```

time: 202 us -> 191 us (0.946)
  the two profiles are of different devices: /device:TPU:162 before, /device:TPU:44 now
where the time goes in v2:
time: 191 us; the launch traced here: 190 us
  Pallas kernels  177 us (93%)
  local copies, waits for them, and re-layouts  6.48 us (3%)
  other arithmetic  6.21 us (3%)
    pallas_call x1, Pallas kernels, local(): pl.pallas_call(local_kernel, out_shape=(jax.ShapeDtypeStruct(slots, bf16)...  177 us

profile of v2, /device:TPU:44, one launch (start us, length us, event | category | flops | bytes accessed | tf_op | source)
XLA Modules:
  0.0 190.3 jit_solution(1797638805579817293)
XLA Ops:
  0.6 0.7 and_select_fusion
  1.3 0.7 fusion.3
  2.0 0.7 bitcast_convert_fusion
  2.6 0.7 convert_bitcast_fusion.1
  3.3 0.6 fusion.rid_ref
  3.9 0.1 copy.16
  4.1 0.1 reduce
  4.2 0.7 fusion.2
  4.8 0.1 convert_reduce_fusion
  4.9 0.5 add_subtract_fusion.pick
  5.4 0.1 add_select_fusion
  5.5 0.6 select_n.20.place
  6.1 0.1 fusion.1
  6.2 0.6 reshape.80.alive
  6.8 177.0 %shard_map.119 = (bf16[8,6,16,512]{3,2,1,0:T(8,128)(2,1)}, f32[8,128]{1,0:T(8,128)}, f32[512,512]{1,0:T(8,128)}, f32[64,512]{1,0:T(8,128)}, f32[64,512]{1,0:T(8,128)}) custom-call(s32[48]{0:T(128)} %add_subtract_fusion.pick, s32[96]{0:T(128)} %select_n.20.place, s32[96]{0:T(128)} %reshape.80.alive, bf16[6,8,16,512]{3,2,1,0:T(8,128)(2,1)} %bitcast.20, ...), custom_call_target="tpu_custom_call" | custom-call | tf_op jit(solution)/shard_map/pallas_call | solution.py:454
  183.8 1.3 slice_bitcast_fusion
  185.0 1.3 convert_bitcast_fusion
  186.4 0.0 copy-start
  186.4 1.3 copy.17
  187.7 0.0 copy-start.2
  187.7 0.0 copy-start.1
  187.7 0.3 copy-done
  188.0 1.0 copy.21
  189.0 0.0 copy-done.2
  189.0 0.7 copy.22
  189.6 0.0 copy-done.1
  189.6 0.7 copy.23
  (1 shorter events, 0.0 us)
Async XLA Ops:
  186.4 1.6 copy-start
  187.7 1.3 copy-start.2
  187.7 2.0 %copy-start.1 = (f32[64,512]{1,0:T(8,128)S(1)}, f32[64,512]{1,0:T(8,128)}, u32[]{:S(2)}) copy-start(f32[64,512]{1,0:T(8,128)} %get-tuple-element.26) | copy-start | bytes 393220

commit v3 on v2

--- a/solution.py
+++ b/solution.py
@@ -257,10 +257,20 @@
                 ring[i, h].reshape(ROWS, HALF), gated_hid[...].reshape(ROWS, WIDTH), contract_rows,
                 preferred_element_type=f32).astype(bf16).reshape(4, PIECE, WIDTH)
 
-        give(w_send.at[i], w_recv.at[chip], wg_send, wg_recv.at[0], 2 * origin + core)
+        def scatter(j, c):
+            d = (chip + j) % CHIPS
+            give(w_send.at[i, d], w_recv.at[i, chip], wg_send, wg_recv.at[i], 2 * d + core)
+            return c
+        lax.fori_loop(0, CHIPS, scatter, 0)
         term = jnp.dot(ring[i, 0].reshape(ROWS, HALF), weights[origin, 0], preferred_element_type=f32)
         term = term + jnp.dot(ring[i, 1].reshape(ROWS, HALF), weights[origin, 1], preferred_element_type=f32)
         pre[...] = pre[...] + term.reshape(GROUPS, GROUP, WIDTH)
+        return c
+
+    def collect(i, c):
+        wait_bytes(w_recv.at[i], wg_recv.at[i])
+        sum_send[i] = jnp.sum(w_recv[i].astype(f32), axis=0).astype(bf16)
+        give(sum_send.at[i], sum_recv.at[chip], sum_sem.at[0], sum_sem.at[1], 2 * origin_of(i) + core)
         return c
 
     def run(i, c):
@@ -315,6 +325,10 @@
                 wait_bytes(ring.at[RING - 1, h], ring_recv.at[RING - 1, h])
 
         compute(i, c)
+
+        @pl.when(i >= 4)
+        def _():
+            collect(i - 4, c)
         return c
     lax.fori_loop(0, RING, run, 0)
 
@@ -362,6 +376,7 @@
         give(h_send.at[d], h_recv.at[chip], hr_sem.at[0], hr_sem.at[1], 2 * d + core)
         return c
     lax.fori_loop(0, CHIPS, give_back, 0)
+    lax.fori_loop(4, RING, collect, 0)
 
     wait_bytes(gate_recv, gate_sem.at[1])
     total = jnp.sum(gate_recv[...], axis=0)
@@ -398,9 +413,8 @@
     dg_out[...] = jnp.sum(g_recv[1].astype(f32), axis=0)
     wait_bytes(h_recv, hr_sem.at[1])
     hg_out[...] = h_recv[...]
-    wait_bytes(w_recv, wg_recv.at[0])
-    for d in range(CHIPS):
-        wg_out[d * PIECE:(d + 1) * PIECE] = jnp.sum(w_recv[:, d].astype(f32), axis=0)
+    wait_bytes(sum_recv, sum_sem.at[1])
+    wg_out[...] = sum_recv[...].reshape(WIDTH, WIDTH).astype(f32)
     wait_bytes(gate_back, gate_sem.at[3])
     gg_out[...] = jnp.sum(gate_back[...], axis=0)
 
@@ -425,6 +439,7 @@
     wait_bytes(proj, p_sem.at[2])
     wait_bytes(g_send.at[pl.ds(0, 15)], gr_sem.at[0])
     wait_bytes(w_send.at[pl.ds(0, 7)], wg_send)
+    wait_bytes(sum_send.at[pl.ds(0, 7)], sum_sem.at[0])
     for d in range(CHIPS):
         to_other(d).wait_send()
     wait_bytes(h_send.at[pl.ds(0, 7)], hr_sem.at[0])

time: 191 us -> 159 us (0.83)
  the two profiles are of different devices: /device:TPU:44 before, /device:TPU:4 now
where the time goes in v3:
time: 159 us; the launch traced here: 158 us
  Pallas kernels  145 us (91%)
  local copies, waits for them, and re-layouts  6.48 us (4%)
  other arithmetic  6.21 us (4%)
    pallas_call x1, Pallas kernels, local(): pl.pallas_call(local_kernel, out_shape=(jax.ShapeDtypeStruct(slots, bf16)...  145 us

profile of v3, /device:TPU:4, one launch (start us, length us, event | category | flops | bytes accessed | tf_op | source)
XLA Modules:
  0.0 158.0 jit_solution(11874486774880594284)
XLA Ops:
  0.6 0.7 and_select_fusion
  1.3 0.7 fusion.3
  2.0 0.7 bitcast_convert_fusion
  2.6 0.7 convert_bitcast_fusion.1
  3.3 0.6 fusion.rid_ref
  3.9 0.1 copy.16
  4.1 0.1 reduce
  4.2 0.7 fusion.2
  4.8 0.1 convert_reduce_fusion
  4.9 0.5 add_subtract_fusion.pick
  5.4 0.1 add_select_fusion
  5.5 0.6 select_n.20.place
  6.1 0.1 fusion.1
  6.2 0.6 reshape.80.alive
  6.8 144.6 %shard_map.119 = (bf16[8,6,16,512]{3,2,1,0:T(8,128)(2,1)}, f32[8,128]{1,0:T(8,128)}, f32[512,512]{1,0:T(8,128)}, f32[64,512]{1,0:T(8,128)}, f32[64,512]{1,0:T(8,128)}) custom-call(s32[48]{0:T(128)} %add_subtract_fusion.pick, s32[96]{0:T(128)} %select_n.20.place, s32[96]{0:T(128)} %reshape.80.alive, bf16[6,8,16,512]{3,2,1,0:T(8,128)(2,1)} %bitcast.20, ...), custom_call_target="tpu_custom_call" | custom-call | tf_op jit(solution)/shard_map/pallas_call | solution.py:469
  151.4 1.3 slice_bitcast_fusion
  152.7 1.3 convert_bitcast_fusion
  154.0 0.0 copy-start
  154.1 1.3 copy.17
  155.3 0.0 copy-start.2
  155.3 0.0 copy-start.1
  155.3 0.3 copy-done
  155.7 1.0 copy.21
  156.6 0.0 copy-done.2
  156.6 0.7 copy.22
  157.3 0.0 copy-done.1
  157.3 0.7 copy.23
  (1 shorter events, 0.0 us)
Async XLA Ops:
  154.0 1.6 %copy-start = (f32[512,512]{1,0:T(8,128)S(1)}, f32[512,512]{1,0:T(8,128)}, u32[]{:S(2)}) copy-start(f32[512,512]{1,0:T(8,128)} %get-tuple-element.24) | copy-start | bytes 3145732
  155.3 1.3 copy-start.2
  155.3 2.0 %copy-start.1 = (f32[64,512]{1,0:T(8,128)S(1)}, f32[64,512]{1,0:T(8,128)}, u32[]{:S(2)}) copy-start(f32[64,512]{1,0:T(8,128)} %get-tuple-element.26) | copy-start | bytes 393220

commit v4 on v2

--- a/solution.py
+++ b/solution.py
@@ -34,10 +34,10 @@
     hg_out, gg_out, wg_out, dg_out, ug_out,
     recv_low, recv_high, recv_rid, slot_gate, slot_depth, gates, depths,
     rows, hid, gated_hid, ring, weights, pre,
-    w_send, w_recv, sum_send, sum_recv, maps, part_send, part_recv, part_sum, proj, wide,
+    w_send, a_recv, b_send, b_recv, sum_send, sum_recv, maps, part_send, part_recv, part_sum, proj, wide,
     g_send, g_recv, x_send, x_recv, h_send, h_recv,
     gate_part, gate_recv, gate_rows, gate_slots, gate_back,
-    in_sem, w_sem, ring_send, ring_recv, hid_sem, p_sem, wg_send, wg_recv, sum_sem,
+    in_sem, w_sem, ring_send, ring_recv, hid_sem, p_sem, wg_send, wg_recv, b_sem, sum_sem, map_sem,
     gr_sem, x_ssem, x_rsem, hr_sem, gate_sem,
 ):
     s = lax.axis_index("seq")
@@ -48,6 +48,8 @@
     xl = t % 2
     is_cot = core == xl
     kind = (core + xl) % 2
+    x_at = chip // 4
+    y_at = chip % 4
     recv_rows = (recv_low, recv_high)
 
     def remote(src, dst, ssem, rsem, seq, tp):
@@ -117,12 +119,11 @@
             return c
         lax.fori_loop(0, CHIPS, send_hid, 0)
 
-        def send_maps(i, c):
-            d = (chip + i) % CHIPS
-            give(up_ref, maps.at[s], in_sem.at[4], in_sem.at[5], 2 * d + xl)
-            give(down_ref, maps.at[s], in_sem.at[4], in_sem.at[5], 2 * d + 1 - xl)
-            return c
-        lax.fori_loop(0, CHIPS, send_maps, 0)
+        for x2 in range(2):
+            d = 4 * ((x_at + x2) % 2) + y_at
+            mine = maps.at[x_at, y_at, core]
+            give(up_ref, mine, in_sem.at[4], in_sem.at[5], 2 * d + xl)
+            give(down_ref, mine, in_sem.at[4], in_sem.at[5], 2 * d + 1 - xl)
 
     right = 2 * ((z + 1) % RING) + xl
     left = 2 * ((z + RING - 1) % RING) + xl
@@ -194,6 +195,13 @@
     lax.fori_loop(0, GROUPS, pack_rid, 0, unroll=4)
     pre[...] = jnp.zeros_like(pre)
 
+    wait_bytes(maps.at[:, 0], in_sem.at[5])
+
+    def to_column(i):
+        d = 4 * x_at + (y_at + i) % 4
+        return remote(maps.at[:, y_at], maps.at[:, y_at], map_sem.at[0], map_sem.at[1], 2 * d + core, t)
+    for i in range(1, 4):
+        to_column(i).start()
     forward(1)
 
     @pl.when(jnp.logical_not(is_cot))
@@ -209,7 +217,7 @@
             lax.fori_loop(0, GROUPS, pack, 0, unroll=4)
         to_partner().start()
 
-    wait_bytes(maps, in_sem.at[5])
+    wait_bytes(maps.at[:, pl.ds(0, 3)], map_sem.at[1])
 
     def project(r, c):
         groups = pl.ds(r * GROUP, GROUP)
@@ -253,14 +261,61 @@
         origin = origin_of(i)
         pltpu.make_async_copy(w_ref.at[0], weights.at[origin], w_sem.at[origin]).wait()
         for h in range(2):
-            w_send[i, h * 4:(h + 1) * 4] = lax.dot_general(
+            w_send[i, h] = lax.dot_general(
                 ring[i, h].reshape(ROWS, HALF), gated_hid[...].reshape(ROWS, WIDTH), contract_rows,
                 preferred_element_type=f32).astype(bf16).reshape(4, PIECE, WIDTH)
 
-        give(w_send.at[i], w_recv.at[chip], wg_send, wg_recv.at[0], 2 * origin + core)
+        @pl.when(i % 2 == 1)
+        def _():
+            remote(w_send.at[i, 1 - x_at], a_recv.at[i, 0], wg_send.at[0], wg_recv.at[i],
+                   2 * (4 * (1 - x_at) + y_at) + core, t).start()
+
+        @pl.when(i % 2 == 0)
+        def _():
+            def scatter(j, c):
+                y2 = (y_at + j) % 4
+                give(w_send.at[i, :, y2], a_recv.at[i, :, y_at], wg_send.at[0], wg_recv.at[i],
+                     2 * (4 * x_at + y2) + core)
+                return c
+            lax.fori_loop(0, 4, scatter, 0)
         term = jnp.dot(ring[i, 0].reshape(ROWS, HALF), weights[origin, 0], preferred_element_type=f32)
         term = term + jnp.dot(ring[i, 1].reshape(ROWS, HALF), weights[origin, 1], preferred_element_type=f32)
         pre[...] = pre[...] + term.reshape(GROUPS, GROUP, WIDTH)
+        return c
+
+    def second(i, c):
+        @pl.when(i % 2 == 1)
+        def _():
+            wait_bytes(a_recv.at[i, 0], wg_recv.at[i])
+            b_send[i] = (w_send[i, x_at].astype(f32) + a_recv[i, 0].astype(f32)).astype(bf16)
+
+            def scatter(j, c):
+                y2 = (y_at + j) % 4
+                give(b_send.at[i, y2], b_recv.at[i, y_at], wg_send.at[1], b_sem.at[i],
+                     2 * (4 * x_at + y2) + core)
+                return c
+            lax.fori_loop(0, 4, scatter, 0)
+
+        @pl.when(i % 2 == 0)
+        def _():
+            wait_bytes(a_recv.at[i], wg_recv.at[i])
+            for x2 in range(2):
+                b_send[i, x2] = jnp.sum(a_recv[i, x2].astype(f32), axis=0).astype(bf16)
+            remote(b_send.at[i, 1 - x_at], b_recv.at[i, 0], wg_send.at[1], b_sem.at[i],
+                   2 * (4 * (1 - x_at) + y_at) + core, t).start()
+        return c
+
+    def third(i, c):
+        @pl.when(i % 2 == 1)
+        def _():
+            wait_bytes(b_recv.at[i], b_sem.at[i])
+            sum_send[i] = jnp.sum(b_recv[i].astype(f32), axis=0).astype(bf16)
+
+        @pl.when(i % 2 == 0)
+        def _():
+            wait_bytes(b_recv.at[i, 0], b_sem.at[i])
+            sum_send[i] = (b_send[i, x_at].astype(f32) + b_recv[i, 0].astype(f32)).astype(bf16)
+        give(sum_send.at[i], sum_recv.at[chip], sum_sem.at[0], sum_sem.at[1], 2 * origin_of(i) + core)
         return c
 
     def run(i, c):
@@ -311,10 +366,21 @@
                 return c
             lax.fori_loop(1, 16, send_grad, 0)
             pltpu.make_async_copy(g_send.at[s], g_recv.at[kind, chip], gr_sem.at[1]).start()
+            lax.fori_loop(5, 7, second, 0)
+            lax.fori_loop(2, 5, third, 0)
             for h in range(2):
                 wait_bytes(ring.at[RING - 1, h], ring_recv.at[RING - 1, h])
 
         compute(i, c)
+
+        @pl.when(i == 4)
+        def _():
+            lax.fori_loop(0, 2, second, 0)
+
+        @pl.when(i == 6)
+        def _():
+            lax.fori_loop(2, 5, second, 0)
+            lax.fori_loop(0, 2, third, 0)
         return c
     lax.fori_loop(0, RING, run, 0)
 
@@ -362,6 +428,9 @@
         give(h_send.at[d], h_recv.at[chip], hr_sem.at[0], hr_sem.at[1], 2 * d + core)
         return c
     lax.fori_loop(0, CHIPS, give_back, 0)
+    lax.fori_loop(5, 7, third, 0)
+    second(RING - 1, 0)
+    third(RING - 1, 0)
 
     wait_bytes(gate_recv, gate_sem.at[1])
     total = jnp.sum(gate_recv[...], axis=0)
@@ -398,16 +467,16 @@
     dg_out[...] = jnp.sum(g_recv[1].astype(f32), axis=0)
     wait_bytes(h_recv, hr_sem.at[1])
     hg_out[...] = h_recv[...]
-    wait_bytes(w_recv, wg_recv.at[0])
-    for d in range(CHIPS):
-        wg_out[d * PIECE:(d + 1) * PIECE] = jnp.sum(w_recv[:, d].astype(f32), axis=0)
+    wait_bytes(sum_recv, sum_sem.at[1])
+    wg_out[...] = sum_recv[...].reshape(WIDTH, WIDTH).astype(f32)
     wait_bytes(gate_back, gate_sem.at[3])
     gg_out[...] = jnp.sum(gate_back[...], axis=0)
 
     for h in range(2):
         wait_bytes(recv_rows[h].at[pl.ds(0, 15 * LEVELS)], in_sem.at[h])
     wait_bytes(recv_rid.at[pl.ds(0, 15)], in_sem.at[2])
-    wait_bytes(maps.at[pl.ds(0, 15)], in_sem.at[4])
+    wait_bytes(maps.at[0, pl.ds(0, 3), 0], in_sem.at[4])
+    wait_bytes(maps.at[:, pl.ds(0, 3)], map_sem.at[0])
 
     @pl.when(is_cot)
     def _():
@@ -424,7 +493,9 @@
     wait_bytes(part_recv.at[pl.ds(0, 15)], p_sem.at[0])
     wait_bytes(proj, p_sem.at[2])
     wait_bytes(g_send.at[pl.ds(0, 15)], gr_sem.at[0])
-    wait_bytes(w_send.at[pl.ds(0, 7)], wg_send)
+    wait_bytes(w_send.at[pl.ds(0, 5)], wg_send.at[0])
+    wait_bytes(b_send.at[pl.ds(0, 4)], wg_send.at[1])
+    wait_bytes(sum_send.at[pl.ds(0, 7)], sum_sem.at[0])
     for d in range(CHIPS):
         to_other(d).wait_send()
     wait_bytes(h_send.at[pl.ds(0, 7)], hr_sem.at[0])
@@ -476,11 +547,13 @@
             pltpu.VMEM((RING, 2, GROUPS, GROUP, HALF), bf16),
             pltpu.VMEM((RING, 2, HALF, WIDTH), bf16),
             pltpu.VMEM(grouped, f32),
-            pltpu.VMEM((RING, CHIPS, PIECE, WIDTH), bf16),
-            pltpu.VMEM((RING, CHIPS, PIECE, WIDTH), bf16),
+            pltpu.VMEM((RING, 2, 4, PIECE, WIDTH), bf16),
+            pltpu.VMEM((RING, 2, 4, PIECE, WIDTH), bf16),
+            pltpu.VMEM((RING, 4, PIECE, WIDTH), bf16),
+            pltpu.VMEM((RING, 4, PIECE, WIDTH), bf16),
             pltpu.VMEM((RING, PIECE, WIDTH), bf16),
             pltpu.VMEM((CHIPS, PIECE, WIDTH), bf16),
-            pltpu.VMEM((16, PIECE, WIDTH), bf16),
+            pltpu.VMEM((2, 4, 2, PIECE, WIDTH), bf16),
             pltpu.VMEM((ROWS, RANK), bf16),
             pltpu.VMEM((PEERS, PART, RANK), bf16),
             pltpu.VMEM((PART, RANK), bf16),
@@ -503,8 +576,10 @@
             dma((RING, 2)),
             dma((2,)),
             dma((4,)),
-            dma,
+            dma((2,)),
             dma((RING,)),
+            dma((RING,)),
+            dma((2,)),
             dma((2,)),
             dma((2,)),
             dma((CHIPS,)),

time: 191 us -> 159 us (0.83)
  the two profiles are of different devices: /device:TPU:44 before, /device:TPU:4 now
where the time goes in v4:
time: 159 us; the launch traced here: 157 us
  Pallas kernels  144 us (91%)
  local copies, waits for them, and re-layouts  6.48 us (4%)
  other arithmetic  6.21 us (4%)
    pallas_call x1, Pallas kernels, local(): pl.pallas_call(local_kernel, out_shape=(jax.ShapeDtypeStruct(slots, bf16)...  144 us

profile of v4, /device:TPU:4, one launch (start us, length us, event | category | flops | bytes accessed | tf_op | source)
XLA Modules:
  0.0 157.0 jit_solution(11822469710004401907)
XLA Ops:
  0.6 0.7 and_select_fusion
  1.3 0.7 fusion.3
  2.0 0.7 bitcast_convert_fusion
  2.6 0.7 convert_bitcast_fusion.1
  3.3 0.6 fusion.rid_ref
  3.9 0.1 copy.16
  4.1 0.1 reduce
  4.2 0.7 fusion.2
  4.8 0.1 convert_reduce_fusion
  4.9 0.5 add_subtract_fusion.pick
  5.4 0.1 add_select_fusion
  5.5 0.6 select_n.20.place
  6.1 0.1 fusion.1
  6.2 0.6 reshape.80.alive
  6.8 143.6 %shard_map.119 = (bf16[8,6,16,512]{3,2,1,0:T(8,128)(2,1)}, f32[8,128]{1,0:T(8,128)}, f32[512,512]{1,0:T(8,128)}, f32[64,512]{1,0:T(8,128)}, f32[64,512]{1,0:T(8,128)}) custom-call(s32[48]{0:T(128)} %add_subtract_fusion.pick, s32[96]{0:T(128)} %select_n.20.place, s32[96]{0:T(128)} %reshape.80.alive, bf16[6,8,16,512]{3,2,1,0:T(8,128)(2,1)} %bitcast.20, ...), custom_call_target="tpu_custom_call" | custom-call | tf_op jit(solution)/shard_map/pallas_call | solution.py:525
  150.4 1.3 slice_bitcast_fusion
  151.7 1.3 convert_bitcast_fusion
  153.0 0.0 copy-start
  153.1 1.3 copy.17
  154.3 0.0 copy-start.2
  154.3 0.0 copy-start.1
  154.3 0.3 copy-done
  154.7 1.0 copy.21
  155.6 0.0 copy-done.2
  155.6 0.7 copy.22
  156.3 0.0 copy-done.1
  156.3 0.7 copy.23
  (1 shorter events, 0.0 us)
Async XLA Ops:
  153.0 1.6 %copy-start = (f32[512,512]{1,0:T(8,128)S(1)}, f32[512,512]{1,0:T(8,128)}, u32[]{:S(2)}) copy-start(f32[512,512]{1,0:T(8,128)} %get-tuple-element.24) | copy-start | bytes 3145732
  154.3 1.3 copy-start.2
  154.3 2.0 %copy-start.1 = (f32[64,512]{1,0:T(8,128)S(1)}, f32[64,512]{1,0:T(8,128)}, u32[]{:S(2)}) copy-start(f32[64,512]{1,0:T(8,128)} %get-tuple-element.26) | copy-start | bytes 393220

commit v5 on v4

--- a/solution.py
+++ b/solution.py
@@ -30,9 +30,9 @@
 
 
 def local_kernel(
-    pick, place, alive, cot_ref, hid_ref, rid_ref, up_ref, down_ref, w_ref,
+    pick, place, cot_ref, hid_ref, gate_ref, depth_ref, up_ref, down_ref, w_ref,
     hg_out, gg_out, wg_out, dg_out, ug_out,
-    recv_low, recv_high, recv_rid, slot_gate, slot_depth, gates, depths,
+    recv_low, recv_high, rid_send, recv_rid, slot_gate, slot_depth, gates, depths,
     rows, hid, gated_hid, ring, weights, pre,
     w_send, a_recv, b_send, b_recv, sum_send, sum_recv, maps, part_send, part_recv, part_sum, proj, wide,
     g_send, g_recv, x_send, x_recv, h_send, h_recv,
@@ -103,27 +103,40 @@
     for h in range(2):
         lax.fori_loop(0, CHIPS, functools.partial(send_first, h), 0)
 
+    rid_send[...] = jnp.zeros_like(rid_send)
+    rid_send[0:LEVELS] = gate_ref[...].astype(f32)
+    rid_send[8:8 + LEVELS] = depth_ref[...].astype(f32)
+
     def send_rid(i, c):
         d = (chip + i) % CHIPS
         for other in range(2):
-            give(rid_ref, recv_rid.at[s], in_sem.at[2], in_sem.at[3], 2 * d + other)
+            give(rid_send, recv_rid.at[s], in_sem.at[2], in_sem.at[3], 2 * d + other)
         return c
     lax.fori_loop(0, CHIPS, send_rid, 0)
 
-    def send_second():
-        def send_hid(i, c):
+    def send_hid():
+        def send(i, c):
             d = (chip + i) % CHIPS
             for h in range(2):
                 give(hid_ref.at[:, d, :, half(h)], recv_rows[h].at[my_slots], in_sem.at[h], in_sem.at[6 + h],
                      2 * d + 1 - xl)
             return c
-        lax.fori_loop(0, CHIPS, send_hid, 0)
-
-        for x2 in range(2):
-            d = 4 * ((x_at + x2) % 2) + y_at
-            mine = maps.at[x_at, y_at, core]
-            give(up_ref, mine, in_sem.at[4], in_sem.at[5], 2 * d + xl)
-            give(down_ref, mine, in_sem.at[4], in_sem.at[5], 2 * d + 1 - xl)
+        lax.fori_loop(0, CHIPS, send, 0)
+
+    for x2 in range(2):
+        d = 4 * ((x_at + x2) % 2) + y_at
+        mine = maps.at[x_at, y_at, core]
+        give(up_ref, mine, in_sem.at[4], in_sem.at[5], 2 * d + xl)
+        give(down_ref, mine, in_sem.at[4], in_sem.at[5], 2 * d + 1 - xl)
+
+    def to_column(i):
+        d = 4 * x_at + (y_at + i) % 4
+        return remote(maps.at[:, y_at], maps.at[:, y_at], map_sem.at[0], map_sem.at[1], 2 * d + core, t)
+
+    def pass_maps():
+        wait_bytes(maps.at[:, 0], in_sem.at[5])
+        for i in range(1, 4):
+            to_column(i).start()
 
     right = 2 * ((z + 1) % RING) + xl
     left = 2 * ((z + RING - 1) % RING) + xl
@@ -167,14 +180,16 @@
             to_across(h).start()
             to_right(ring.at[0, h], 1, h).start()
             to_left(ring.at[0, h], 2, h).start()
+        pass_maps()
 
     @pl.when(jnp.logical_not(is_cot))
     def _():
+        pass_maps()
         for h in range(2):
             wait_bytes(ring.at[0, h], ring_recv.at[0, h])
             to_right(ring.at[0, h], 1, h).start()
             to_left(ring.at[0, h], 2, h).start()
-    send_second()
+    send_hid()
 
     wait_bytes(recv_rid, in_sem.at[3])
     lane = lax.broadcasted_iota(jnp.int32, (GROUP, BLOCK), 1)
@@ -195,13 +210,6 @@
     lax.fori_loop(0, GROUPS, pack_rid, 0, unroll=4)
     pre[...] = jnp.zeros_like(pre)
 
-    wait_bytes(maps.at[:, 0], in_sem.at[5])
-
-    def to_column(i):
-        d = 4 * x_at + (y_at + i) % 4
-        return remote(maps.at[:, y_at], maps.at[:, y_at], map_sem.at[0], map_sem.at[1], 2 * d + core, t)
-    for i in range(1, 4):
-        to_column(i).start()
     forward(1)
 
     @pl.when(jnp.logical_not(is_cot))
@@ -322,6 +330,22 @@
         @pl.when(i == 3)
         def _():
             forward(3)
+
+        @pl.when(i == 5)
+        def _():
+            forward(5)
+
+        @pl.when(i == RING - 1)
+        def _():
+            lax.fori_loop(5, 7, second, 0)
+            lax.fori_loop(2, 5, third, 0)
+            for h in range(2):
+                wait_bytes(ring.at[RING - 1, h], ring_recv.at[RING - 1, h])
+
+        compute(i, c)
+
+        @pl.when(i == 4)
+        def _():
             wait_bytes(part_recv, p_sem.at[1])
             part_sum[...] = jnp.sum(part_recv[...].astype(f32), axis=0).astype(bf16)
 
@@ -331,13 +355,12 @@
                        4 * chip + 1 - same_kind(t2), t2).start()
                 return c
             lax.fori_loop(0, PEERS, send_sum, 0)
-
-        @pl.when(i == 5)
-        def _():
-            forward(5)
-
-        @pl.when(i == RING - 1)
-        def _():
+            lax.fori_loop(0, 2, second, 0)
+
+        @pl.when(i == 6)
+        def _():
+            lax.fori_loop(2, 5, second, 0)
+            lax.fori_loop(0, 2, third, 0)
             wait_bytes(proj, p_sem.at[3])
             flat = proj[...].reshape(ROWS, RANK)
             depth = depths[...].reshape(ROWS, BLOCK)[:, 0:1]
@@ -366,21 +389,6 @@
                 return c
             lax.fori_loop(1, 16, send_grad, 0)
             pltpu.make_async_copy(g_send.at[s], g_recv.at[kind, chip], gr_sem.at[1]).start()
-            lax.fori_loop(5, 7, second, 0)
-            lax.fori_loop(2, 5, third, 0)
-            for h in range(2):
-                wait_bytes(ring.at[RING - 1, h], ring_recv.at[RING - 1, h])
-
-        compute(i, c)
-
-        @pl.when(i == 4)
-        def _():
-            lax.fori_loop(0, 2, second, 0)
-
-        @pl.when(i == 6)
-        def _():
-            lax.fori_loop(2, 5, second, 0)
-            lax.fori_loop(0, 2, third, 0)
         return c
     lax.fori_loop(0, RING, run, 0)
 
@@ -406,7 +414,8 @@
 
     def slot_rows(slot):
         gate = slot_gate[slot][:, 0:1]
-        return jnp.where(alive[slot] > 0, gate * pre[place[slot]], 0.0)
+        at = place[slot]
+        return jnp.where(at >= 0, gate * pre[jnp.maximum(at, 0)], 0.0)
 
     def to_other(d):
         return remote(x_send.at[d], x_recv.at[d], x_ssem.at[d], x_rsem.at[d], partner, t)
@@ -428,9 +437,8 @@
         give(h_send.at[d], h_recv.at[chip], hr_sem.at[0], hr_sem.at[1], 2 * d + core)
         return c
     lax.fori_loop(0, CHIPS, give_back, 0)
-    lax.fori_loop(5, 7, third, 0)
     second(RING - 1, 0)
-    third(RING - 1, 0)
+    lax.fori_loop(5, RING, third, 0)
 
     wait_bytes(gate_recv, gate_sem.at[1])
     total = jnp.sum(gate_recv[...], axis=0)
@@ -452,7 +460,8 @@
         lines = []
         for j in range(LEVELS):
             slot = (2 * d + core) * LEVELS + j
-            value = jnp.where(alive[slot] > 0, gate_rows[place[slot]], 0.0)
+            at = place[slot]
+            value = jnp.where(at >= 0, gate_rows[jnp.maximum(at, 0)], 0.0)
             lines.append(jnp.where(mine, value, 0.0))
         gate_slots[d] = jnp.concatenate(lines + [jnp.zeros((2, BLOCK), f32)], axis=0)
 
@@ -466,9 +475,10 @@
     ug_out[...] = jnp.sum(g_recv[0].astype(f32), axis=0)
     dg_out[...] = jnp.sum(g_recv[1].astype(f32), axis=0)
     wait_bytes(h_recv, hr_sem.at[1])
-    hg_out[...] = h_recv[...]
+    for d in range(CHIPS):
+        hg_out[:, d] = h_recv[d]
     wait_bytes(sum_recv, sum_sem.at[1])
-    wg_out[...] = sum_recv[...].reshape(WIDTH, WIDTH).astype(f32)
+    wg_out[...] = sum_recv[...].reshape(WIDTH, WIDTH)
     wait_bytes(gate_back, gate_sem.at[3])
     gg_out[...] = jnp.sum(gate_back[...], axis=0)
 
@@ -504,20 +514,16 @@
 
 
 def local(hidden, cotangent, router_gate, recursion_depth, live_counts, out_weight, adapter_down, adapter_up):
-    rider = jnp.stack([router_gate.astype(f32), recursion_depth.astype(f32)]).reshape(2, LEVELS, BLOCK)
-    rider = jnp.pad(rider, ((0, 0), (0, 2), (0, 0))).reshape(16, BLOCK)
     split = (LEVELS, CHIPS, GROUP, WIDTH)
-    blocks = live_counts // BLOCK
-    finish = jnp.cumsum(blocks)
-    begin = finish - blocks
-    level = jnp.arange(LEVELS, dtype=jnp.int32)
-    alive = level[None, :] < blocks[:, None]
-    place = jnp.where(alive, begin[:, None] + level[None, :], 0)
+    blocks = lax.shift_right_logical(live_counts, 7)
+    slot = jnp.arange(96, dtype=jnp.int32)
+    shard = jnp.arange(16, dtype=jnp.int32)
+    owner = (slot // LEVELS)[:, None]
+    before = jnp.sum(jnp.where(shard[None, :] < owner, blocks[None, :], 0), axis=1)
+    own = jnp.sum(jnp.where(shard[None, :] == owner, blocks[None, :], 0), axis=1)
+    place = jnp.where(slot % LEVELS < own, before + slot % LEVELS, -1)
     order = jnp.arange(GROUPS, dtype=jnp.int32)
-    past = finish[None, :] <= order[:, None]
-    source = jnp.sum(past.astype(jnp.int32), axis=1)
-    first = jnp.max(jnp.where(past, finish[None, :], 0), axis=1)
-    pick = source * LEVELS + order - first
+    pick = jnp.sum(jnp.where(place[None, :] == order[:, None], slot[None, :], 0), axis=1)
     vmem = pl.BlockSpec(memory_space=pltpu.VMEM)
     grouped = (GROUPS, GROUP, WIDTH)
     slots = (CHIPS, LEVELS, GROUP, WIDTH)
@@ -525,17 +531,18 @@
     out = pl.pallas_call(
         local_kernel,
         out_shape=(
-            jax.ShapeDtypeStruct(slots, bf16),
+            jax.ShapeDtypeStruct(split, bf16),
             jax.ShapeDtypeStruct((8, BLOCK), f32),
-            jax.ShapeDtypeStruct((WIDTH, WIDTH), f32),
+            jax.ShapeDtypeStruct((WIDTH, WIDTH), bf16),
             jax.ShapeDtypeStruct((PIECE, WIDTH), f32),
             jax.ShapeDtypeStruct((PIECE, WIDTH), f32),
         ),
-        in_specs=[pl.BlockSpec(memory_space=pltpu.SMEM)] * 3 + [vmem] * 5 + [pl.BlockSpec(memory_space=pl.ANY)],
+        in_specs=[pl.BlockSpec(memory_space=pltpu.SMEM)] * 2 + [vmem] * 6 + [pl.BlockSpec(memory_space=pl.ANY)],
         out_specs=(vmem,) * 5,
         scratch_shapes=[
             pltpu.VMEM((96, GROUP, HALF), bf16),
             pltpu.VMEM((96, GROUP, HALF), bf16),
+            pltpu.VMEM((16, BLOCK), f32),
             pltpu.VMEM((16, 16, BLOCK), f32),
             pltpu.VMEM((96, GROUP, BLOCK), f32),
             pltpu.VMEM((96, GROUP, BLOCK), f32),
@@ -591,12 +598,13 @@
             collective_id=0, has_side_effects=True, vmem_limit_bytes=VMEM_LIMIT
         ),
     )(
-        pick, place.reshape(96), alive.reshape(96).astype(jnp.int32), cotangent.reshape(split), hidden.reshape(split), rider,
+        pick, place, cotangent.reshape(split), hidden.reshape(split),
+        router_gate.reshape(LEVELS, BLOCK), recursion_depth.reshape(LEVELS, BLOCK),
         adapter_up, adapter_down.T, out_weight.reshape(PEERS, 2, HALF, WIDTH),
     )
     hidden_grad, gate_back, weight_grad, down_grad, up_grad = out
-    hidden_grad = hidden_grad.transpose(1, 0, 2, 3).reshape(hidden.shape).astype(f32)
-    return hidden_grad, gate_back[:LEVELS].reshape(-1), weight_grad, down_grad, up_grad
+    hidden_grad = hidden_grad.reshape(hidden.shape).astype(f32)
+    return hidden_grad, gate_back[:LEVELS].reshape(-1), weight_grad.astype(f32), down_grad, up_grad
 
 
 def solution(mesh):

time: 159 us -> 151 us (0.950); the launches traced: 157 us -> 151 us
  local copies, waits for them, and re-layouts: 6.48 us -> 2.65 us
    convert_element_type x2, other arithmetic: 1.4 us -> 3.64 us  [the longest x1 2.53 us: local(): hidden_grad = hidden_grad.reshape(hidden.shape).astype(f32)]
    another operation x5 -> x0, other arithmetic: 2.19 us -> none  [the longest x2 1.37 us: local(): jnp.stack([router_gate.astype(f32), recursion_depth.astype(f32)])]
    convert_element_type x2 -> x0, local copies, waits for them, and re-layouts: 1.88 us -> none  [the longest x1 1.28 us: local(): hidden_grad.transpose(1, 0, 2, 3).reshape(hidden.shape).astype(f32)]
where the time goes in v5:
time: 151 us
  Pallas kernels  143 us (95%)
  other arithmetic  5.03 us (3%)
  local copies, waits for them, and re-layouts  2.65 us (2%)
    pallas_call x1, Pallas kernels, local(): pl.pallas_call(local_kernel, out_shape=(jax.ShapeDtypeStruct(split, bf16)...  143 us

profile of v5, /device:TPU:4, one launch (start us, length us, event | category | flops | bytes accessed | tf_op | source)
XLA Modules:
  0.0 151.2 jit_solution(10533223376250237052)
XLA Ops:
  0.6 0.7 broadcast_shift-right-logical_fusion
  1.3 0.1 select_reduce_fusion.1
  1.4 0.0 copy-start.3
  1.4 0.6 select_reduce_fusion.pick
  2.0 0.0 copy-done.3
  2.0 142.9 %shard_map.119 = (bf16[6,8,16,512]{3,2,1,0:T(8,128)(2,1)}, f32[8,128]{1,0:T(8,128)}, bf16[512,512]{1,0:T(8,128)(2,1)}, f32[64,512]{1,0:T(8,128)}, f32[64,512]{1,0:T(8,128)}) custom-call(s32[48]{0:T(128)} %select_reduce_fusion.pick, s32[96]{0:T(128)} %copy-done.3, bf16[6,8,16,512]{3,2,1,0:T(8,128)(2,1)} %bitcast.12, bf16[6,8,16,512]{3,2,1,0:T(8,128)(2,1)} %bitcast.13, ...), custom_call_target="tpu_custom_call" | custom-call | tf_op jit(solution)/shard_map/pallas_call | solution.py:531
  144.9 0.0 copy-start
  144.9 1.3 slice_bitcast_fusion
  146.3 0.0 copy-start.2
  146.3 0.0 copy-start.1
  146.3 2.5 %bitcast_convert_fusion = f32[768,512]{1,0:T(8,128)} fusion(bf16[6,8,16,512]{3,2,1,0:T(8,128)(2,1)} %get-tuple-element.10), kind=kLoop, calls=%fused_computation | loop fusion | flops 393216 | bytes 2359296 | tf_op jit(solution)/shard_map/convert_element_type | solution.py:606
  148.8 0.0 copy-done
  148.8 1.1 convert_element_type.11
  149.9 0.0 copy-done.2
  149.9 0.7 copy.15
  150.6 0.0 copy-done.1
  150.6 0.7 copy.16
  (2 shorter events, 0.0 us)
Async XLA Ops:
  1.4 0.6 copy-start.3
  144.9 3.9 %copy-start = (bf16[512,512]{1,0:T(8,128)(2,1)S(1)}, bf16[512,512]{1,0:T(8,128)(2,1)}, u32[]{:S(2)}) copy-start(bf16[512,512]{1,0:T(8,128)(2,1)} %get-tuple-element.12) | copy-start | bytes 1572868
  146.3 3.6 %copy-start.2 = (f32[64,512]{1,0:T(8,128)S(1)}, f32[64,512]{1,0:T(8,128)}, u32[]{:S(2)}) copy-start(f32[64,512]{1,0:T(8,128)} %get-tuple-element.25) | copy-start | bytes 393220
  146.3 4.3 %copy-start.1 = (f32[64,512]{1,0:T(8,128)S(1)}, f32[64,512]{1,0:T(8,128)}, u32[]{:S(2)}) copy-start(f32[64,512]{1,0:T(8,128)} %get-tuple-element.26) | copy-start | bytes 393220

commit v6 on v5

--- a/solution.py
+++ b/solution.py
@@ -326,6 +326,17 @@
         give(sum_send.at[i], sum_recv.at[chip], sum_sem.at[0], sum_sem.at[1], 2 * origin_of(i) + core)
         return c
 
+    def sum_parts():
+        wait_bytes(part_recv, p_sem.at[1])
+        part_sum[...] = jnp.sum(part_recv[...].astype(f32), axis=0).astype(bf16)
+
+        def send_sum(j, c):
+            t2 = (t + j) % PEERS
+            remote(part_sum, proj.at[t], p_sem.at[2], p_sem.at[3],
+                   4 * chip + 1 - same_kind(t2), t2).start()
+            return c
+        lax.fori_loop(0, PEERS, send_sum, 0)
+
     def run(i, c):
         @pl.when(i == 3)
         def _():
@@ -346,15 +357,7 @@
 
         @pl.when(i == 4)
         def _():
-            wait_bytes(part_recv, p_sem.at[1])
-            part_sum[...] = jnp.sum(part_recv[...].astype(f32), axis=0).astype(bf16)
-
-            def send_sum(j, c):
-                t2 = (t + j) % PEERS
-                remote(part_sum, proj.at[t], p_sem.at[2], p_sem.at[3],
-                       4 * chip + 1 - same_kind(t2), t2).start()
-                return c
-            lax.fori_loop(0, PEERS, send_sum, 0)
+            pl.when(jnp.logical_not(is_cot))(sum_parts)
             lax.fori_loop(0, 2, second, 0)
 
         @pl.when(i == 6)
@@ -390,6 +393,7 @@
             lax.fori_loop(1, 16, send_grad, 0)
             pltpu.make_async_copy(g_send.at[s], g_recv.at[kind, chip], gr_sem.at[1]).start()
         return c
+    pl.when(is_cot)(sum_parts)
     lax.fori_loop(0, RING, run, 0)
 
     ones = jnp.ones((8, WIDTH), bf16)
@@ -437,9 +441,8 @@
         give(h_send.at[d], h_recv.at[chip], hr_sem.at[0], hr_sem.at[1], 2 * d + core)
         return c
     lax.fori_loop(0, CHIPS, give_back, 0)
+    lax.fori_loop(5, 7, third, 0)
     second(RING - 1, 0)
-    lax.fori_loop(5, RING, third, 0)
-
     wait_bytes(gate_recv, gate_sem.at[1])
     total = jnp.sum(gate_recv[...], axis=0)
     group_of = lax.shift_right_logical(lax.broadcasted_iota(jnp.int32, (GROUPS, ROWS), 1), 4)
@@ -470,6 +473,7 @@
         give(gate_slots.at[d], gate_back.at[chip], gate_sem.at[2], gate_sem.at[3], 2 * d + core)
         return c
     lax.fori_loop(0, CHIPS, give_slots, 0)
+    third(RING - 1, 0)
 
     wait_bytes(g_recv, gr_sem.at[1])
     ug_out[...] = jnp.sum(g_recv[0].astype(f32), axis=0)

time: 151 us -> 150 us (level)
  Pallas kernels: 143 us -> 141 us
    pallas_call x1, Pallas kernels: 143 us -> 141 us  [local(): pl.pallas_call(local_kernel, out_shape=(jax.ShapeDtypeStruct(split, bf16)...]
where the time goes in v6:
time: 150 us
  Pallas kernels  141 us (94%)
  other arithmetic  5.03 us (3%)
  local copies, waits for them, and re-layouts  2.65 us (2%)
    pallas_call x1, Pallas kernels, local(): pl.pallas_call(local_kernel, out_shape=(jax.ShapeDtypeStruct(split, bf16)...  141 us

profile of v6, /device:TPU:4, one launch (start us, length us, event | category | flops | bytes accessed | tf_op | source)
XLA Modules:
  0.0 149.6 jit_solution(286956404167777264)
XLA Ops:
  0.6 0.7 broadcast_shift-right-logical_fusion
  1.3 0.1 select_reduce_fusion.1
  1.4 0.0 copy-start.3
  1.4 0.6 select_reduce_fusion.pick
  2.0 0.0 copy-done.3
  2.0 141.2 %shard_map.119 = (bf16[6,8,16,512]{3,2,1,0:T(8,128)(2,1)}, f32[8,128]{1,0:T(8,128)}, bf16[512,512]{1,0:T(8,128)(2,1)}, f32[64,512]{1,0:T(8,128)}, f32[64,512]{1,0:T(8,128)}) custom-call(s32[48]{0:T(128)} %select_reduce_fusion.pick, s32[96]{0:T(128)} %copy-done.3, bf16[6,8,16,512]{3,2,1,0:T(8,128)(2,1)} %bitcast.12, bf16[6,8,16,512]{3,2,1,0:T(8,128)(2,1)} %bitcast.13, ...), custom_call_target="tpu_custom_call" | custom-call | tf_op jit(solution)/shard_map/pallas_call | solution.py:535
  143.3 0.0 copy-start
  143.3 1.3 slice_bitcast_fusion
  144.6 0.0 copy-start.2
  144.6 0.0 copy-start.1
  144.6 2.5 %bitcast_convert_fusion = f32[768,512]{1,0:T(8,128)} fusion(bf16[6,8,16,512]{3,2,1,0:T(8,128)(2,1)} %get-tuple-element.10), kind=kLoop, calls=%fused_computation | loop fusion | flops 393216 | bytes 2359296 | tf_op jit(solution)/shard_map/convert_element_type | solution.py:610
  147.2 0.0 copy-done
  147.2 1.1 convert_element_type.11
  148.3 0.0 copy-done.2
  148.3 0.7 copy.15
  148.9 0.0 copy-done.1
  148.9 0.7 copy.16
  (2 shorter events, 0.0 us)
Async XLA Ops:
  1.4 0.6 copy-start.3
  143.3 3.9 %copy-start = (bf16[512,512]{1,0:T(8,128)(2,1)S(1)}, bf16[512,512]{1,0:T(8,128)(2,1)}, u32[]{:S(2)}) copy-start(bf16[512,512]{1,0:T(8,128)(2,1)} %get-tuple-element.12) | copy-start | bytes 1572868
  144.6 3.6 %copy-start.2 = (f32[64,512]{1,0:T(8,128)S(1)}, f32[64,512]{1,0:T(8,128)}, u32[]{:S(2)}) copy-start(f32[64,512]{1,0:T(8,128)} %get-tuple-element.25) | copy-start | bytes 393220
  144.6 4.3 %copy-start.1 = (f32[64,512]{1,0:T(8,128)S(1)}, f32[64,512]{1,0:T(8,128)}, u32[]{:S(2)}) copy-start(f32[64,512]{1,0:T(8,128)} %get-tuple-element.26) | copy-start | bytes 393220

commit v7 on v6

--- a/solution.py
+++ b/solution.py
@@ -337,6 +337,36 @@
             return c
         lax.fori_loop(0, PEERS, send_sum, 0)
 
+    def grads():
+        wait_bytes(proj, p_sem.at[3])
+        flat = proj[...].reshape(ROWS, RANK)
+        depth = depths[...].reshape(ROWS, BLOCK)[:, 0:1]
+        for d in range(NREC):
+            wide[:, d * RANK:(d + 1) * RANK] = jnp.where(
+                depth == d + 1.0, 0.5 * flat.astype(f32), 0.0).astype(bf16)
+
+        @pl.when(jnp.logical_not(is_cot))
+        def _():
+            def add_adapter(r, c):
+                groups = pl.ds(r * GROUP, GROUP)
+                term = jnp.dot(wide[pl.ds(r * RANK, RANK)], maps[...].reshape(NREC * RANK, WIDTH),
+                               preferred_element_type=f32)
+                pre[groups] = pre[groups] + term.reshape(GROUP, GROUP, WIDTH)
+                return c
+            lax.fori_loop(0, ROWS // RANK, add_adapter, 0)
+
+        for q in range(NREC):
+            grad = lax.dot_general(wide[:, q * RANK:(q + 1) * RANK], rows[...].reshape(ROWS, WIDTH),
+                                   contract_rows, preferred_element_type=f32)
+            g_send[q * 4:(q + 1) * 4] = grad.astype(bf16).reshape(4, PIECE, WIDTH)
+
+        def send_grad(j, c):
+            to = (s + j) % 16
+            remote(g_send.at[to], g_recv.at[kind, chip], gr_sem.at[0], gr_sem.at[1], to, t).start()
+            return c
+        lax.fori_loop(1, 16, send_grad, 0)
+        pltpu.make_async_copy(g_send.at[s], g_recv.at[kind, chip], gr_sem.at[1]).start()
+
     def run(i, c):
         @pl.when(i == 3)
         def _():
@@ -350,6 +380,7 @@
         def _():
             lax.fori_loop(5, 7, second, 0)
             lax.fori_loop(2, 5, third, 0)
+            pl.when(is_cot)(grads)
             for h in range(2):
                 wait_bytes(ring.at[RING - 1, h], ring_recv.at[RING - 1, h])
 
@@ -359,39 +390,12 @@
         def _():
             pl.when(jnp.logical_not(is_cot))(sum_parts)
             lax.fori_loop(0, 2, second, 0)
+            pl.when(jnp.logical_not(is_cot))(grads)
 
         @pl.when(i == 6)
         def _():
             lax.fori_loop(2, 5, second, 0)
             lax.fori_loop(0, 2, third, 0)
-            wait_bytes(proj, p_sem.at[3])
-            flat = proj[...].reshape(ROWS, RANK)
-            depth = depths[...].reshape(ROWS, BLOCK)[:, 0:1]
-            for d in range(NREC):
-                wide[:, d * RANK:(d + 1) * RANK] = jnp.where(
-                    depth == d + 1.0, 0.5 * flat.astype(f32), 0.0).astype(bf16)
-
-            @pl.when(jnp.logical_not(is_cot))
-            def _():
-                def add_adapter(r, c):
-                    groups = pl.ds(r * GROUP, GROUP)
-                    term = jnp.dot(wide[pl.ds(r * RANK, RANK)], maps[...].reshape(NREC * RANK, WIDTH),
-                                   preferred_element_type=f32)
-                    pre[groups] = pre[groups] + term.reshape(GROUP, GROUP, WIDTH)
-                    return c
-                lax.fori_loop(0, ROWS // RANK, add_adapter, 0)
-
-            for q in range(NREC):
-                grad = lax.dot_general(wide[:, q * RANK:(q + 1) * RANK], rows[...].reshape(ROWS, WIDTH),
-                                       contract_rows, preferred_element_type=f32)
-                g_send[q * 4:(q + 1) * 4] = grad.astype(bf16).reshape(4, PIECE, WIDTH)
-
-            def send_grad(j, c):
-                to = (s + j) % 16
-                remote(g_send.at[to], g_recv.at[kind, chip], gr_sem.at[0], gr_sem.at[1], to, t).start()
-                return c
-            lax.fori_loop(1, 16, send_grad, 0)
-            pltpu.make_async_copy(g_send.at[s], g_recv.at[kind, chip], gr_sem.at[1]).start()
         return c
     pl.when(is_cot)(sum_parts)
     lax.fori_loop(0, RING, run, 0)

time: 150 us -> 146 us (0.973)
  Pallas kernels: 141 us -> 137 us
    pallas_call x1, Pallas kernels: 141 us -> 137 us  [local(): pl.pallas_call(local_kernel, out_shape=(jax.ShapeDtypeStruct(split, bf16)...]
where the time goes in v7:
time: 146 us
  Pallas kernels  137 us (94%)
  other arithmetic  5.03 us (3%)
  local copies, waits for them, and re-layouts  2.65 us (2%)
    pallas_call x1, Pallas kernels, local(): pl.pallas_call(local_kernel, out_shape=(jax.ShapeDtypeStruct(split, bf16)...  137 us

profile of v7, /device:TPU:4, one launch (start us, length us, event | category | flops | bytes accessed | tf_op | source)
XLA Modules:
  0.0 145.7 jit_solution(9160027401099222227)
XLA Ops:
  0.6 0.7 broadcast_shift-right-logical_fusion
  1.3 0.1 select_reduce_fusion.1
  1.4 0.0 copy-start.3
  1.4 0.6 select_reduce_fusion.pick
  2.0 0.0 copy-done.3
  2.0 137.3 %shard_map.119 = (bf16[6,8,16,512]{3,2,1,0:T(8,128)(2,1)}, f32[8,128]{1,0:T(8,128)}, bf16[512,512]{1,0:T(8,128)(2,1)}, f32[64,512]{1,0:T(8,128)}, f32[64,512]{1,0:T(8,128)}) custom-call(s32[48]{0:T(128)} %select_reduce_fusion.pick, s32[96]{0:T(128)} %copy-done.3, bf16[6,8,16,512]{3,2,1,0:T(8,128)(2,1)} %bitcast.12, bf16[6,8,16,512]{3,2,1,0:T(8,128)(2,1)} %bitcast.13, ...), custom_call_target="tpu_custom_call" | custom-call | tf_op jit(solution)/shard_map/pallas_call | solution.py:539
  139.4 0.0 copy-start
  139.4 1.3 slice_bitcast_fusion
  140.7 0.0 copy-start.2
  140.7 0.0 copy-start.1
  140.7 2.5 %bitcast_convert_fusion = f32[768,512]{1,0:T(8,128)} fusion(bf16[6,8,16,512]{3,2,1,0:T(8,128)(2,1)} %get-tuple-element.10), kind=kLoop, calls=%fused_computation | loop fusion | flops 393216 | bytes 2359296 | tf_op jit(solution)/shard_map/convert_element_type | solution.py:614
  143.3 0.0 copy-done
  143.3 1.1 convert_element_type.11
  144.4 0.0 copy-done.2
  144.4 0.7 copy.15
  145.0 0.0 copy-done.1
  145.0 0.7 copy.16
  (2 shorter events, 0.0 us)
Async XLA Ops:
  1.4 0.6 copy-start.3
  139.4 3.9 %copy-start = (bf16[512,512]{1,0:T(8,128)(2,1)S(1)}, bf16[512,512]{1,0:T(8,128)(2,1)}, u32[]{:S(2)}) copy-start(bf16[512,512]{1,0:T(8,128)(2,1)} %get-tuple-element.12) | copy-start | bytes 1572868
  140.7 3.6 %copy-start.2 = (f32[64,512]{1,0:T(8,128)S(1)}, f32[64,512]{1,0:T(8,128)}, u32[]{:S(2)}) copy-start(f32[64,512]{1,0:T(8,128)} %get-tuple-element.25) | copy-start | bytes 393220
  140.7 4.3 %copy-start.1 = (f32[64,512]{1,0:T(8,128)S(1)}, f32[64,512]{1,0:T(8,128)}, u32[]{:S(2)}) copy-start(f32[64,512]{1,0:T(8,128)} %get-tuple-element.26) | copy-start | bytes 393220

commit v8 on v7

--- a/solution.py
+++ b/solution.py
@@ -380,11 +380,14 @@
         def _():
             lax.fori_loop(5, 7, second, 0)
             lax.fori_loop(2, 5, third, 0)
-            pl.when(is_cot)(grads)
             for h in range(2):
                 wait_bytes(ring.at[RING - 1, h], ring_recv.at[RING - 1, h])
 
         compute(i, c)
+
+        @pl.when(i == RING - 1)
+        def _():
+            pl.when(is_cot)(grads)
 
         @pl.when(i == 4)
         def _():

time: 146 us -> 145 us (level)
  no operation moved by 1% of the time
where the time goes in v8:
time: 145 us
  Pallas kernels  136 us (94%)
  other arithmetic  5.03 us (3%)
  local copies, waits for them, and re-layouts  2.65 us (2%)
    pallas_call x1, Pallas kernels, local(): pl.pallas_call(local_kernel, out_shape=(jax.ShapeDtypeStruct(split, bf16)...  136 us

profile of v8, /device:TPU:4, one launch (start us, length us, event | category | flops | bytes accessed | tf_op | source)
XLA Modules:
  0.0 144.6 jit_solution(15872919142991432984)
XLA Ops:
  0.6 0.7 broadcast_shift-right-logical_fusion
  1.3 0.1 select_reduce_fusion.1
  1.4 0.0 copy-start.3
  1.4 0.6 select_reduce_fusion.pick
  2.0 0.0 copy-done.3
  2.0 136.2 %shard_map.119 = (bf16[6,8,16,512]{3,2,1,0:T(8,128)(2,1)}, f32[8,128]{1,0:T(8,128)}, bf16[512,512]{1,0:T(8,128)(2,1)}, f32[64,512]{1,0:T(8,128)}, f32[64,512]{1,0:T(8,128)}) custom-call(s32[48]{0:T(128)} %select_reduce_fusion.pick, s32[96]{0:T(128)} %copy-done.3, bf16[6,8,16,512]{3,2,1,0:T(8,128)(2,1)} %bitcast.12, bf16[6,8,16,512]{3,2,1,0:T(8,128)(2,1)} %bitcast.13, ...), custom_call_target="tpu_custom_call" | custom-call | tf_op jit(solution)/shard_map/pallas_call | solution.py:542
  138.3 0.0 copy-start
  138.3 1.3 slice_bitcast_fusion
  139.6 0.0 copy-start.2
  139.6 0.0 copy-start.1
  139.6 2.5 %bitcast_convert_fusion = f32[768,512]{1,0:T(8,128)} fusion(bf16[6,8,16,512]{3,2,1,0:T(8,128)(2,1)} %get-tuple-element.10), kind=kLoop, calls=%fused_computation | loop fusion | flops 393216 | bytes 2359296 | tf_op jit(solution)/shard_map/convert_element_type | solution.py:617
  142.1 0.0 copy-done
  142.1 1.1 convert_element_type.11
  143.2 0.0 copy-done.2
  143.2 0.7 copy.15
  143.9 0.0 copy-done.1
  143.9 0.7 copy.16
  (2 shorter events, 0.0 us)
Async XLA Ops:
  1.4 0.6 copy-start.3
  138.3 3.9 %copy-start = (bf16[512,512]{1,0:T(8,128)(2,1)S(1)}, bf16[512,512]{1,0:T(8,128)(2,1)}, u32[]{:S(2)}) copy-start(bf16[512,512]{1,0:T(8,128)(2,1)} %get-tuple-element.12) | copy-start | bytes 1572868
  139.6 3.6 %copy-start.2 = (f32[64,512]{1,0:T(8,128)S(1)}, f32[64,512]{1,0:T(8,128)}, u32[]{:S(2)}) copy-start(f32[64,512]{1,0:T(8,128)} %get-tuple-element.25) | copy-start | bytes 393220
  139.6 4.3 %copy-start.1 = (f32[64,512]{1,0:T(8,128)S(1)}, f32[64,512]{1,0:T(8,128)}, u32[]{:S(2)}) copy-start(f32[64,512]{1,0:T(8,128)} %get-tuple-element.26) | copy-start | bytes 393220
